TPU v7x, 256 devices: a whole 4x4x8 slice. The times are simulated.
256 devices in a mesh: seq: 64 (over z, y, core), batch: 4 (over x).
Axes of the slice: x: 4, y: 4, z: 8, core: 2. Of those that a mesh axis runs over, the one named last changes fastest.
Arguments:
- tokens: bfloat16 [32768, 1440], P(('batch', 'seq')), parts along dimension 0, may hold values from -6 to 6
- norm_gain: float32 [1440], replicated, may hold values from 0.1 to 1.9
- qkv_weight: bfloat16 [1440, 2560], P(None, 'seq'), may hold values from -2 to 2
- sinks: float32 [32], replicated, may hold values from 0 to 5
- out_weight: bfloat16 [2048, 1440], P('seq'), may hold values from -0.125 to 0.125
- moe_gain: float32 [1440], replicated, may hold values from 0.1 to 1.9
- expert_in: bfloat16 [64, 1440, 2880], P('seq'), may hold values from -0.15625 to 0.15625
- expert_out: bfloat16 [64, 1440, 1440], P('seq'), may hold values from -0.15625 to 0.15625
- expert_ids: int32 [32768, 4], P(('batch', 'seq')), parts along dimension 0, may hold values from 0 to 63, all different within a row; in each aligned block of 128 rows (0 to 127, 128 to 255, ...) at most 16 rows name the same one
- gate_ints: int32 [32768, 4], P(('batch', 'seq')), parts along dimension 0, may hold values from 1 to 4096
Outputs:
- block_out: bfloat16 [32768, 1440], P(('batch', 'seq')), parts along dimension 0
There are 4 independent parts, one for each index of `batch`. A program takes and returns all parts, laid end to end along the dimension named above; an argument that names none is the same for every part. Nothing has to cross between parts.
Inputs may be any that keep to these rules, and one draw needn't show every extreme that they name: `expert_ids`: each row names 4 different experts; among the 128 rows of one device no expert is named more than 16 times.
All inputs are finite; a program needn't handle non-finite values.
Results may differ from a plain program's by a relative error of at most 0.012.
Values may be sent and summed in bfloat16 or wider, within the bound.
No kernel may reach another device: no remote copies, remote signals or barrier semaphores. Data moves between devices by JAX's collectives and lax.ppermute only.
A program may use at most 128 MiB of HBM per device.

v0:
```python
import math

import jax
import jax.numpy as jnp
from jax import lax
from jax.experimental import pallas as pl
from jax.experimental.pallas import tpu as pltpu
from jax.sharding import Mesh
from jax.sharding import PartitionSpec as P

QH = 32
KVH = 4
HD = 64
WIN = 128
TOP = 4


epsilon = 1e-05
rope_base = 150000.0
glu_slope = 1.702
SEQ = ("z", "y", "c")
PLANE = ("y", "c")
CAP = 16
META = 3 * TOP
TILE = 128
SPAN = 384
VMEM_LIMIT = 48 * 1024 * 1024


def shifted(value, axis, steps):
    count = math.prod(lax.axis_size(name) for name in axis)
    initial, last = (max(0, -steps), min(count, count - steps))
    return lax.ppermute(value, axis, [(source, source + steps) for source in range(initial, last)])


def norm_scale(values, gain):
    widened = values.astype(jnp.float32)
    mean_sq = jnp.mean(widened * widened, axis=-1, keepdims=True)
    return widened * lax.rsqrt(mean_sq + epsilon) * gain


def rotate(values, positions):
    half_width = values.shape[-1] // 2
    freq_steps = jnp.arange(half_width).astype(jnp.float32)
    inverse = jnp.exp(freq_steps * (-2.0 * math.log(rope_base) / values.shape[-1]))
    angles = positions[:, None] * inverse[None, :]
    cosine = jnp.cos(angles)[:, None, :]
    sine_term = jnp.sin(angles)[:, None, :]
    lower_half = values[..., :half_width]
    second = values[..., half_width:]
    return jnp.concatenate(
        [lower_half * cosine - second * sine_term, second * cosine + lower_half * sine_term],
        axis=-1,
    )


def band_block(queries, key_heads, value_heads, sinks, first_pos):
    count = queries.shape[0]
    groups = QH // KVH
    grouped = queries.reshape(count, KVH, groups, HD)
    scores = jnp.einsum(
        "tkgd,skd->kgts", grouped, key_heads, preferred_element_type=jnp.float32
    ) * (1.0 / math.sqrt(HD))
    query_pos = first_pos + jnp.arange(count)
    key_pos = first_pos - count + jnp.arange(2 * count)
    distance = query_pos[:, None] - key_pos[None, :]
    allowed = (distance >= 0) & (distance < WIN) & (key_pos >= 0)[None, :]
    scores = jnp.where(allowed[None, None, :, :], scores, -jnp.inf)
    sink_logit = sinks.reshape(KVH, groups, 1, 1)
    row_peak = jnp.maximum(jnp.max(scores, axis=-1, keepdims=True), sink_logit)
    raised = jnp.exp(scores - row_peak)
    totals = jnp.sum(raised, axis=-1, keepdims=True) + jnp.exp(sink_logit - row_peak)
    weights = (raised / totals).astype(jnp.bfloat16)
    mixture = jnp.einsum("kgts,skd->tkgd", weights, value_heads, preferred_element_type=jnp.float32)
    return mixture.reshape(count, QH * HD).astype(jnp.bfloat16)


def whole(count):
    return [pl.BlockSpec(memory_space=pltpu.VMEM)] * count


def local_call(body, out_shape, in_specs, scratch_shapes=()):
    outs = jax.tree.leaves(out_shape)
    return pl.pallas_call(
        body,
        out_shape=out_shape,
        in_specs=in_specs,
        out_specs=jax.tree.map(lambda _: pl.BlockSpec(memory_space=pltpu.VMEM), out_shape)
        if len(outs) > 1
        else pl.BlockSpec(memory_space=pltpu.VMEM),
        scratch_shapes=scratch_shapes,
        compiler_params=pltpu.CompilerParams(vmem_limit_bytes=VMEM_LIMIT),
    )


def slot_match(meta, first_expert, which):
    ids = meta[:, which : which + 1] - first_expert
    places = ids * float(CAP) + meta[:, TOP + which : TOP + which + 1]
    columns = lax.broadcasted_iota(jnp.int32, (meta.shape[0], 8 * CAP), 1).astype(jnp.float32)
    return columns == places


def select_rows(block, width, first_expert):
    meta = block[:, width : width + META].astype(jnp.float32)
    pick = jnp.zeros((block.shape[0], 8 * CAP), jnp.float32)
    for which in range(TOP):
        pick = jnp.where(slot_match(meta, first_expert, which), 1.0, pick)
    return lax.dot_general(
        pick.astype(jnp.bfloat16),
        block[:, :width],
        (((0,), (0,)), ((), ())),
        preferred_element_type=jnp.float32,
    ).astype(jnp.bfloat16)


def weigh_rows(block, width, first_expert, rows):
    meta = block[:, width : width + META].astype(jnp.float32)
    share = jnp.zeros((block.shape[0], 8 * CAP), jnp.float32)
    for which in range(TOP):
        share = jnp.where(
            slot_match(meta, first_expert, which),
            meta[:, 2 * TOP + which : 2 * TOP + which + 1],
            share,
        )
    return jnp.dot(share.astype(jnp.bfloat16), rows, preferred_element_type=jnp.float32)


def dispatch_rows(plane, blocks, width):
    count = len(blocks)

    def body(plane_ref, *refs):
        out_ref = refs[-1]
        first_expert = (plane_ref[0] * 8).astype(jnp.float32)
        for number in range(count):
            rows = select_rows(refs[number][...], width, first_expert)
            out_ref[:, number * CAP : (number + 1) * CAP, :] = rows.reshape(8, CAP, width)

    return local_call(
        body,
        jax.ShapeDtypeStruct((8, count * CAP, width), jnp.bfloat16),
        [pl.BlockSpec(memory_space=pltpu.SMEM)] + whole(count),
    )(plane, *blocks)


def run_expert(groups, parts, weight_in, weight_out):
    width = groups[0].shape[-1]
    hidden = weight_out.shape[1]
    total = sum(8 * group.shape[1] for group in groups)
    tiles = total // TILE
    count_in = width // SPAN
    rest = count_in * SPAN
    shapes = [(8, size, width) for sizes in parts for size in sizes]

    def body(*refs):
        ins, (in_hbm, out_hbm) = refs[: len(groups)], refs[len(groups) : len(groups) + 2]
        outs = refs[len(groups) + 2 : len(groups) + 2 + len(shapes)]
        in_ref, out_ref, rows_ref, acc_ref, sems = refs[len(groups) + 2 + len(shapes) :]

        def fetch(low, size, sem):
            return pltpu.make_async_copy(
                in_hbm.at[0, pl.ds(low, size)], in_ref.at[pl.ds(low, size)], sems.at[sem]
            )

        last = fetch(rest, width - rest, count_in)
        last.start()
        for n in range(count_in):
            fetch(n * SPAN, SPAN, n).start()
        down = pltpu.make_async_copy(out_hbm.at[0], out_ref, sems.at[count_in + 1])
        down.start()
        start = 0
        for rows in ins:
            count = 8 * rows.shape[1]
            rows_ref[start : start + count] = rows[...].reshape(count, width)
            start += count
        last.wait()

        def first(tile, carry):
            at = pl.ds(pl.multiple_of(tile * TILE, TILE), TILE)
            acc_ref[at] = jnp.dot(
                rows_ref[at, rest:], in_ref[rest:], preferred_element_type=jnp.float32
            )
            return carry

        lax.fori_loop(0, tiles, first, 0)

        def more(n, carry):
            low = pl.multiple_of(n * SPAN, SPAN)
            fetch(low, SPAN, n).wait()

            def multiply(tile, carry):
                at = pl.ds(pl.multiple_of(tile * TILE, TILE), TILE)
                acc_ref[at] += jnp.dot(
                    rows_ref[at, pl.ds(low, SPAN)],
                    in_ref[pl.ds(low, SPAN)],
                    preferred_element_type=jnp.float32,
                )
                return carry

            return lax.fori_loop(0, tiles, multiply, carry)

        lax.fori_loop(0, count_in, more, 0)
        down.wait()

        def finish(tile, carry):
            at = pl.ds(pl.multiple_of(tile * TILE, TILE), TILE)
            gate_part = acc_ref[at, :hidden]
            up_part = acc_ref[at, hidden:]
            activated = (
                gate_part * (1.0 / (1.0 + jnp.exp(-glu_slope * gate_part))) * (up_part + 1.0)
            ).astype(jnp.bfloat16)
            rows_ref[at] = jnp.dot(
                activated, out_ref[...], preferred_element_type=jnp.float32
            ).astype(jnp.bfloat16)
            return carry

        lax.fori_loop(0, tiles, finish, 0)
        start, place = 0, 0
        for group, sizes in zip(ins, parts):
            count = 8 * group.shape[1]
            made = rows_ref[start : start + count].reshape(8, group.shape[1], width)
            at = 0
            for size in sizes:
                outs[place][...] = made[:, at : at + size]
                at += size
                place += 1
            start += count

    return pl.pallas_call(
        body,
        out_shape=[jax.ShapeDtypeStruct(shape, jnp.bfloat16) for shape in shapes],
        in_specs=whole(len(groups)) + [pl.BlockSpec(memory_space=pltpu.HBM)] * 2,
        out_specs=whole(len(shapes)),
        scratch_shapes=[
            pltpu.VMEM((width, 2 * hidden), jnp.bfloat16),
            pltpu.VMEM((hidden, width), jnp.bfloat16),
            pltpu.VMEM((total, width), jnp.bfloat16),
            pltpu.VMEM((total, 2 * hidden), jnp.float32),
            pltpu.SemaphoreType.DMA((count_in + 2,)),
        ],
        compiler_params=pltpu.CompilerParams(vmem_limit_bytes=VMEM_LIMIT),
    )(*groups, weight_in, weight_out)


def project_in(tokens, gain, gathered, depth):
    count, width = tokens.shape
    shards = gathered.shape[0]
    chunks = 4
    step = shards // chunks

    def body(tokens_ref, gain_ref, gathered_hbm, out_ref, weight_ref, sems):
        copies = [
            pltpu.make_async_copy(
                gathered_hbm.at[pl.ds(n * step, step), pl.ds(0, depth)],
                weight_ref.at[pl.ds(n * step, step)],
                sems.at[n],
            )
            for n in range(chunks)
        ]
        for copy in copies:
            copy.start()
        normed = norm_scale(tokens_ref[...], gain_ref[...]).astype(jnp.bfloat16)
        for n, copy in enumerate(copies):
            copy.wait()
            weight = weight_ref[n * step : (n + 1) * step].reshape(step * depth, width)
            out_ref[:, n * step * depth : (n + 1) * step * depth] = lax.dot_general(
                normed, weight, (((1,), (1,)), ((), ())), preferred_element_type=jnp.float32
            )

    return pl.pallas_call(
        body,
        out_shape=jax.ShapeDtypeStruct((count, shards * depth), jnp.float32),
        in_specs=whole(2) + [pl.BlockSpec(memory_space=pltpu.HBM)],
        out_specs=pl.BlockSpec(memory_space=pltpu.VMEM),
        scratch_shapes=[
            pltpu.VMEM((shards, depth, width), jnp.bfloat16),
            pltpu.SemaphoreType.DMA((chunks,)),
        ],
        compiler_params=pltpu.CompilerParams(vmem_limit_bytes=VMEM_LIMIT),
    )(tokens, gain.reshape(1, width), gathered)


def project_out(attention, gathered, skip, tokens, gain, columns):
    count, width = tokens.shape
    shards, depth = gathered.shape[0], gathered.shape[1] - skip
    chunks = 4
    step = shards // chunks

    def body(attention_ref, gathered_hbm, tokens_ref, gain_ref, columns_ref, *refs):
        residual_ref, own_ref, weight_ref, sems = refs
        copies = [
            pltpu.make_async_copy(
                gathered_hbm.at[pl.ds(n * step, step), pl.ds(skip, depth)],
                weight_ref.at[pl.ds(n * step, step)],
                sems.at[n],
            )
            for n in range(chunks)
        ]
        for copy in copies:
            copy.start()
        total = tokens_ref[...].astype(jnp.float32)
        for n, copy in enumerate(copies):
            copy.wait()
            total += jnp.dot(
                attention_ref[:, n * step * depth : (n + 1) * step * depth],
                weight_ref[n * step : (n + 1) * step].reshape(step * depth, width),
                preferred_element_type=jnp.float32,
            )
        middle = total.astype(jnp.bfloat16)
        residual_ref[...] = middle
        own_ref[:, :width] = norm_scale(middle, gain_ref[...]).astype(jnp.bfloat16)
        own_ref[:, width:] = columns_ref[...]

    return pl.pallas_call(
        body,
        out_shape=[
            jax.ShapeDtypeStruct((count, width), jnp.bfloat16),
            jax.ShapeDtypeStruct((count, width + columns.shape[1]), jnp.bfloat16),
        ],
        in_specs=whole(1) + [pl.BlockSpec(memory_space=pltpu.HBM)] + whole(3),
        out_specs=whole(2),
        scratch_shapes=[
            pltpu.VMEM((shards, depth, width), jnp.bfloat16),
            pltpu.SemaphoreType.DMA((chunks,)),
        ],
        compiler_params=pltpu.CompilerParams(vmem_limit_bytes=VMEM_LIMIT),
    )(attention, gathered, tokens, gain.reshape(1, width), columns)


def combine_far(plane, block, rows, width):
    half = block.shape[0] // 2

    def body(plane_ref, block_ref, rows_ref, low_ref, high_ref):
        first_expert = (plane_ref[0] * 8).astype(jnp.float32)
        summed = weigh_rows(
            block_ref[...], width, first_expert, rows_ref[:, -CAP:, :].reshape(8 * CAP, width)
        ).astype(jnp.bfloat16)
        low_ref[...] = summed[:half]
        high_ref[...] = summed[half:]

    return local_call(
        body,
        [jax.ShapeDtypeStruct((half, width), jnp.bfloat16)] * 2,
        [pl.BlockSpec(memory_space=pltpu.SMEM)] + whole(2),
    )(plane, block, rows)


def combine_pair(plane, blocks, rows, arrived, width):
    count = blocks[0].shape[0]

    def body(plane_ref, low_ref, high_ref, rows_ref, first_ref, second_ref, *outs):
        first_expert = (plane_ref[0] * 8).astype(jnp.float32)
        for number, (block, came) in enumerate(((low_ref, first_ref), (high_ref, second_ref))):
            part = rows_ref[:, number * CAP : (number + 1) * CAP, :].reshape(8 * CAP, width)
            summed = weigh_rows(block[...], width, first_expert, part)
            size = came.shape[0]
            if size == count:
                outs[number][...] = (summed + came[...].astype(jnp.float32)).astype(jnp.bfloat16)
            else:
                at = number * size
                other = size - at
                outs[number][at : at + size] = (
                    summed[at : at + size] + came[...].astype(jnp.float32)
                ).astype(jnp.bfloat16)
                outs[number][other : other + size] = summed[other : other + size].astype(
                    jnp.bfloat16
                )

    return local_call(
        body,
        [jax.ShapeDtypeStruct((count, width), jnp.bfloat16)] * 2,
        [pl.BlockSpec(memory_space=pltpu.SMEM)] + whole(5),
    )(plane, *blocks, rows, *arrived)


def combine_last(plane, block, rows, arrived, residual_mid, width):
    def body(plane_ref, block_ref, rows_ref, first_ref, second_ref, residual_ref, out_ref):
        first_expert = (plane_ref[0] * 8).astype(jnp.float32)
        summed = weigh_rows(
            block_ref[...], width, first_expert, rows_ref[...].reshape(8 * CAP, width)
        )
        out_ref[...] = (
            residual_ref[...].astype(jnp.float32)
            + summed
            + first_ref[...].astype(jnp.float32)
            + second_ref[...].astype(jnp.float32)
        ).astype(jnp.bfloat16)

    return local_call(
        body,
        jax.ShapeDtypeStruct(residual_mid.shape, jnp.bfloat16),
        [pl.BlockSpec(memory_space=pltpu.SMEM)] + whole(5),
    )(plane, block, rows, *arrived, residual_mid)


def routing_columns(expert_ids, gate_ints, experts):
    rows = expert_ids.shape[0]
    flat_ids = expert_ids.reshape(-1)
    onehot = (flat_ids[:, None] == jnp.arange(experts)[None, :]).astype(jnp.int32)
    before = jnp.cumsum(onehot, axis=0) - onehot
    slot_index = jnp.sum(before * onehot, axis=1).reshape(rows, TOP)
    route_weight = gate_ints.astype(jnp.float32)
    route_weight = route_weight / jnp.sum(route_weight, axis=-1, keepdims=True)
    return jnp.concatenate(
        [expert_ids.astype(jnp.float32), slot_index.astype(jnp.float32), route_weight], axis=1
    ).astype(jnp.bfloat16)


def local(
    tokens,
    norm_gain,
    qkv_weight,
    sinks,
    out_weight,
    moe_gain,
    expert_in,
    expert_out,
    expert_ids,
    gate_ints,
):
    local_rows = tokens.shape[0]
    width = tokens.shape[1]
    devices = math.prod(lax.axis_size(name) for name in SEQ)
    device_index = lax.axis_index(SEQ)
    query_cols = QH * HD
    key_cols = KVH * HD
    qkv_part = qkv_weight.shape[1]

    both = jnp.concatenate([qkv_weight.T, out_weight], axis=0)
    gathered = lax.all_gather(both, SEQ, axis=0)
    projections = project_in(tokens, norm_gain, gathered, qkv_part)
    first_pos = device_index * local_rows
    positions = (first_pos + jnp.arange(local_rows)).astype(jnp.float32)
    queries = rotate(projections[:, :query_cols].reshape(local_rows, QH, HD), positions).astype(
        jnp.bfloat16
    )
    key_heads = rotate(
        projections[:, query_cols : query_cols + key_cols].reshape(local_rows, KVH, HD), positions
    ).astype(jnp.bfloat16)
    value_heads = (
        projections[:, query_cols + key_cols :].reshape(local_rows, KVH, HD).astype(jnp.bfloat16)
    )
    prev_keys, prev_values = shifted((key_heads, value_heads), SEQ, 1)
    key_block = jnp.concatenate([prev_keys, key_heads], axis=0)
    value_block = jnp.concatenate([prev_values, value_heads], axis=0)
    attention = band_block(queries, key_block, value_block, sinks, first_pos)
    columns = routing_columns(expert_ids, gate_ints, devices)
    residual_mid, own = project_out(
        attention,
        gathered,
        qkv_part,
        tokens,
        moe_gain,
        columns,
    )

    planes = lax.axis_size("z")
    half = local_rows // 2
    plane = lax.axis_index("z").astype(jnp.int32).reshape(1)
    forward = [(at, (at + 1) % planes) for at in range(planes)]
    backward = [(at, (at - 1) % planes) for at in range(planes)]

    def plane_exchange(rows):
        return lax.all_to_all(rows, PLANE, split_axis=0, concat_axis=0, tiled=True)

    weight_in = pltpu.with_memory_space_constraint(expert_in, pltpu.HBM)
    weight_out = pltpu.with_memory_space_constraint(expert_out, pltpu.HBM)

    def pass_on(rows, perm):
        return lax.ppermute(rows, "z", perm)

    rising, falling = [own], [own]
    for _ in range(3):
        rising.append(pass_on(rising[-1], forward))
        falling.append(pass_on(falling[-1], backward))
    far = jnp.concatenate(
        [pass_on(rising[3][:half], forward), pass_on(falling[3][half:], backward)],
        axis=0,
    )
    picked = (
        [own, rising[1], falling[1]],
        [rising[2], falling[2]],
        [rising[3], falling[3], far],
    )
    sent = []
    for group in picked:
        rows = dispatch_rows(plane, group, width)
        sent.append(plane_exchange(rows))
    made_0, made_1, made_2 = run_expert(
        sent[:2], ((CAP, 2 * CAP), (2 * CAP,)), weight_in, weight_out
    )
    (made_3,) = run_expert(sent[2:], ((3 * CAP,),), weight_in, weight_out)
    back = [plane_exchange(rows) for rows in (made_0, made_1, made_2, made_3)]

    to_rising, to_falling = combine_far(plane, far, back[3], width)
    for step in (3, 2, 1):
        to_rising = pass_on(to_rising, backward)
        to_falling = pass_on(to_falling, forward)
        to_rising, to_falling = combine_pair(
            plane,
            (rising[step], falling[step]),
            back[step],
            (to_rising, to_falling),
            width,
        )
    to_rising = pass_on(to_rising, backward)
    to_falling = pass_on(to_falling, forward)
    return combine_last(plane, own, back[0], (to_rising, to_falling), residual_mid, width)


def solution(mesh):
    grid = Mesh(mesh.devices.reshape(8, 4, 2, 4), ("z", "y", "c", "x"))
    rows = P(("x", *SEQ), None)
    return jax.shard_map(
        local,
        mesh=grid,
        in_specs=(
            rows,
            P(),
            P(None, SEQ),
            P(),
            P(SEQ, None),
            P(),
            P(SEQ, None, None),
            P(SEQ, None, None),
            rows,
            rows,
        ),
        out_specs=rows,
        check_vma=False,
    )
```

profile of v0, /device:TPU:1, one launch (start us, length us, event | category | flops | bytes accessed | tf_op | source)
XLA Modules:
  0.0 318.4 jit_solution(11248754453263237922)
XLA Ops:
  17.1 90.2 %all-gather.3.cloned.1.call-done = bf16[4608,1440]{1,0:T(8,128)(2,1)} async-done(((bf16[72,1440]{1,0:T(8,128)(2,1)}), bf16[4608,1440]{1,0:T(8,128)(2,1)}) %all-gather.3.cloned.1.call-update) | async-done | bytes 13271056 | tf_op jit(solution)/shard_map/all_gather | solution.py:429
  107.3 5.0 %shard_map.100 = f32[128,2560]{1,0:T(8,128)S(1)} custom-call(bf16[128,1440]{1,0:T(8,128)(2,1)S(1)} %copy.71.tokens_ref, f32[1,1440]{1,0:T(1,128)S(1)} %reshape.176.gain_ref, bf16[64,72,1440]{2,1,0:T(8,128)(2,1)} %bitcast.53), custom_call_target="tpu_custom_call" | custom-call | tf_op jit(solution)/shard_map/pallas_call | solution.py:269
  112.6 2.0 collective-permute-start
  115.1 2.1 collective-permute-start.1
  121.8 3.4 %shard_map.101 = (bf16[128,1440]{1,0:T(8,128)(2,1)S(1)}, bf16[128,1452]{1,0:T(8,128)(2,1)S(1)}) custom-call(bf16[128,2048]{1,0:T(8,128)(2,1)S(1)} %copy.82.attention_ref, bf16[64,72,1440]{2,1,0:T(8,128)(2,1)} %bitcast.54, bf16[128,1440]{1,0:T(8,128)(2,1)S(1)} %copy.71.tokens_ref, f32[1,1440]{1,0:T(1,128)S(1)} %reshape.179.gain_ref, ...), custom_call_target="tpu_custom_call" | custom-call | tf_op jit(solution)/shard_map/pallas_call | solution.py:313
  126.7 2.0 collective-permute-start.3
  128.7 6.4 %collective-permute-done.2.refs_1_.low_ref = bf16[128,1452]{1,0:T(8,128)(2,1)S(1)} collective-permute-done((bf16[128,1452]{1,0:T(8,128)(2,1)S(1)}, bf16[128,1452]{1,0:T(8,128)(2,1)S(1)}, u32[]{:S(2)}, u32[]{:S(2)}) %collective-permute-start.2) | collective-permute-done | bytes 371744 | tf_op jit(solution)/shard_map/ppermute | solution.py:469
  135.1 2.7 collective-permute-start.5
  137.8 5.6 %collective-permute-done.4.refs_0_.low_ref = bf16[128,1452]{1,0:T(8,128)(2,1)S(1)} collective-permute-done((bf16[128,1452]{1,0:T(8,128)(2,1)S(1)}, bf16[128,1452]{1,0:T(8,128)(2,1)S(1)}, u32[]{:S(2)}, u32[]{:S(2)}) %collective-permute-start.4) | collective-permute-done | bytes 371744 | tf_op jit(solution)/shard_map/ppermute | solution.py:469
  143.3 2.1 shard_map.102
  146.2 12.2 %all-to-all-start = ((bf16[8,48,1440]{2,1,0:T(8,128)(2,1)}), bf16[8,48,1440]{2,1,0:T(8,128)(2,1)S(1)}, u32[]{:S(2)}, u32[]{:S(2)}) async-start(bf16[8,48,1440]{2,1,0:T(8,128)(2,1)} %shard_map.102), calls=%async_computation | async-start | bytes 2359296 | tf_op jit(solution)/shard_map/all_to_all | solution.py:463
  158.4 2.9 collective-permute-start.7
  161.4 8.7 %collective-permute-done.7.refs_1_.high_ref = bf16[128,1452]{1,0:T(8,128)(2,1)S(1)} collective-permute-done((bf16[128,1452]{1,0:T(8,128)(2,1)S(1)}, bf16[128,1452]{1,0:T(8,128)(2,1)S(1)}, u32[]{:S(2)}, u32[]{:S(2)}) %collective-permute-start.7) | collective-permute-done | bytes 371744 | tf_op jit(solution)/shard_map/ppermute | solution.py:469
  170.1 3.2 collective-permute-start.9
  173.2 4.2 %collective-permute-done.9 = bf16[64,1452]{1,0:T(8,128)(2,1)S(1)} collective-permute-done((bf16[64,1452]{1,0:T(8,128)(2,1)S(1)}, bf16[64,1452]{1,0:T(8,128)(2,1)S(1)}, u32[]{:S(2)}, u32[]{:S(2)}) %collective-permute-start.9) | collective-permute-done | bytes 185888 | tf_op jit(solution)/shard_map/ppermute | solution.py:469
  177.4 2.1 shard_map.105
  180.3 5.4 %all-to-all-start.5 = ((bf16[8,48,1440]{2,1,0:T(8,128)(2,1)}), bf16[8,48,1440]{2,1,0:T(8,128)(2,1)S(1)}, u32[]{:S(2)}, u32[]{:S(2)}) async-start(bf16[8,48,1440]{2,1,0:T(8,128)(2,1)} %shard_map.105), calls=%async_computation.5 | async-start | bytes 2359296 | tf_op jit(solution)/shard_map/all_to_all | solution.py:463
  187.4 14.7 %all-to-all-done.5.refs_0_ = bf16[8,48,1440]{2,1,0:T(8,128)(2,1)S(1)} async-done(((bf16[8,48,1440]{2,1,0:T(8,128)(2,1)}), bf16[8,48,1440]{2,1,0:T(8,128)(2,1)S(1)}, u32[]{:S(2)}, u32[]{:S(2)}) %all-to-all-start.5) | async-done | bytes 1105952 | tf_op jit(solution)/shard_map/all_to_all | solution.py:463
  202.1 4.4 %all-to-all-start.1 = ((bf16[8,32,1440]{2,1,0:T(8,128)(2,1)}), bf16[8,32,1440]{2,1,0:T(8,128)(2,1)S(1)}, u32[]{:S(2)}, u32[]{:S(2)}) async-start(bf16[8,32,1440]{2,1,0:T(8,128)(2,1)} %copy-done), calls=%async_computation.1 | async-start | bytes 1572864 | tf_op jit(solution)/shard_map/all_to_all | solution.py:463
  206.5 12.3 %shard_map.106 = bf16[8,48,1440]{2,1,0:T(8,128)(2,1)} custom-call(bf16[8,48,1440]{2,1,0:T(8,128)(2,1)S(1)} %all-to-all-done.5.refs_0_, bf16[1,1440,2880]{2,1,0:T(8,128)(2,1)} %refs_1_.1, bf16[1,1440,1440]{2,1,0:T(8,128)(2,1)} %refs_2_.3), custom_call_target="tpu_custom_call" | custom-call | tf_op jit(solution)/shard_map/pallas_call | solution.py:228
  218.8 4.8 %all-to-all-start.6 = ((bf16[8,48,1440]{2,1,0:T(8,128)(2,1)}), bf16[8,48,1440]{2,1,0:T(8,128)(2,1)S(1)}, u32[]{:S(2)}, u32[]{:S(2)}) async-start(bf16[8,48,1440]{2,1,0:T(8,128)(2,1)} %shard_map.106), calls=%async_computation.6 | async-start | bytes 2359296 | tf_op jit(solution)/shard_map/all_to_all | solution.py:463
  223.6 17.6 %shard_map.104 = (bf16[8,16,1440]{2,1,0:T(8,128)(2,1)S(1)}, bf16[8,32,1440]{2,1,0:T(8,128)(2,1)S(1)}, bf16[8,32,1440]{2,1,0:T(8,128)(2,1)S(1)}) custom-call(bf16[8,48,1440]{2,1,0:T(8,128)(2,1)S(1)} %all-to-all-done.refs_0_, bf16[8,32,1440]{2,1,0:T(8,128)(2,1)S(1)} %all-to-all-done.1.refs_1_, bf16[1,1440,2880]{2,1,0:T(8,128)(2,1)} %refs_1_.1, ...), custom_call_target="tpu_custom_call" | custom-call | tf_op jit(solution)/shard_map/pallas_call | solution.py:228
  243.8 4.8 %all-to-all-start.4 = ((bf16[8,32,1440]{2,1,0:T(8,128)(2,1)}), bf16[8,32,1440]{2,1,0:T(8,128)(2,1)S(1)}, u32[]{:S(2)}, u32[]{:S(2)}) async-start(bf16[8,32,1440]{2,1,0:T(8,128)(2,1)} %copy-done.16), calls=%async_computation.4 | async-start | bytes 1572864 | tf_op jit(solution)/shard_map/all_to_all | solution.py:463
  250.2 3.0 collective-permute-start.10
  253.7 5.2 %collective-permute-done.10.first_ref = bf16[64,1440]{1,0:T(8,128)(2,1)S(1)} collective-permute-done((bf16[64,1440]{1,0:T(8,128)(2,1)S(1)}, bf16[64,1440]{1,0:T(8,128)(2,1)S(1)}, u32[]{:S(2)}, u32[]{:S(2)}) %collective-permute-start.10) | collective-permute-done | bytes 184352 | tf_op jit(solution)/shard_map/ppermute | solution.py:469
  264.6 6.1 %all-to-all-start.3 = ((bf16[8,32,1440]{2,1,0:T(8,128)(2,1)}), bf16[8,32,1440]{2,1,0:T(8,128)(2,1)S(1)}, u32[]{:S(2)}, u32[]{:S(2)}) async-start(bf16[8,32,1440]{2,1,0:T(8,128)(2,1)} %copy-done.15), calls=%async_computation.3 | async-start | bytes 1572864 | tf_op jit(solution)/shard_map/all_to_all | solution.py:463
  270.7 2.2 collective-permute-done.12.first_ref
  277.6 3.1 collective-permute-start.14
  280.7 2.2 all-to-all-done.3.rows_ref
  282.9 4.9 %collective-permute-done.14.first_ref = bf16[128,1440]{1,0:T(8,128)(2,1)S(1)} collective-permute-done((bf16[128,1440]{1,0:T(8,128)(2,1)}, bf16[128,1440]{1,0:T(8,128)(2,1)S(1)}, u32[]{:S(2)}, u32[]{:S(2)}) %collective-permute-start.14) | collective-permute-done | bytes 368672 | tf_op jit(solution)/shard_map/ppermute | solution.py:469
  287.8 2.8 collective-permute-done.15.second_ref
  293.9 15.1 %all_to_all.35.rows_ref = bf16[8,16,1440]{2,1,0:T(8,128)(2,1)S(1)} all-to-all(bf16[8,16,1440]{2,1,0:T(8,128)(2,1)} %copy-done.19), channel_id=1, replica_groups=mesh['z'=8,'y'=4,'c'=2,'x'=4] {'y','c'}, dimensions={0} | all-to-all | bytes 737280 | tf_op jit(solution)/shard_map/all_to_all | solution.py:463
  (121 shorter events, 41.3 us)
Async XLA Ops:
  6.5 100.8 %all-gather.3.cloned.1.call-start = ((), (), s32[]{:S(2)}) async-start(), calls=%async_computation.7 | async-start | bytes 14376960 | tf_op jit(solution)/shard_map/all_gather | solution.py:429
  112.6 7.8 %collective-permute-start = (bf16[128,4,64]{0,2,1:T(8,128)(2,1)S(1)}, bf16[128,4,64]{0,2,1:T(8,128)(2,1)S(1)}, u32[]{:S(2)}, u32[]{:S(2)}) collective-permute-start(bf16[128,4,64]{0,2,1:T(8,128)(2,1)S(1)} %bitcast.61), channel_id=1, source_target_pairs={{0,4},{4,8},{8,12},{12,16},{16,20},{20,24},{24,28},{28,32},{32,36}... | collective-permute-start | bytes 196616 | tf_op jit(solution)/shard_map/ppermute | solution.py:33
  115.1 3.5 %collective-permute-start.1 = (bf16[128,4,64]{0,2,1:T(8,128)(2,1)S(1)}, bf16[128,4,64]{0,2,1:T(8,128)(2,1)S(1)}, u32[]{:S(2)}, u32[]{:S(2)}) collective-permute-start(bf16[128,4,64]{0,2,1:T(8,128)(2,1)S(1)} %pad_maximum_fusion.1), channel_id=1, source_target_pairs={{0,4},{4,8},{8,12},{12,16},{16,20},{20,24},{24,28},{28,32},{32,36}... | collective-permute-start | bytes 196616 | tf_op jit(solution)/shard_map/ppermute | solution.py:33
  126.0 20.2 %copy-start.5 = (bf16[128,1452]{1,0:T(8,128)(2,1)}, bf16[128,1452]{1,0:T(8,128)(2,1)S(1)}, u32[]{:S(2)}) copy-start(bf16[128,1452]{1,0:T(8,128)(2,1)S(1)} %get-tuple-element.18.refs_0_.block_ref) | copy-start | bytes 1115140
  126.0 9.1 %collective-permute-start.2 = (bf16[128,1452]{1,0:T(8,128)(2,1)S(1)}, bf16[128,1452]{1,0:T(8,128)(2,1)S(1)}, u32[]{:S(2)}, u32[]{:S(2)}) collective-permute-start(bf16[128,1452]{1,0:T(8,128)(2,1)S(1)} %get-tuple-element.18.refs_0_.block_ref), channel_id=1, source_target_pairs={{0,32},{32,64},{64,96},{96,128},{128,160},{160,192},{192,224},{224... | collective-permute-start | bytes 1115144 | tf_op jit(solution)/shard_map/ppermute | solution.py:469
  126.7 8.4 %collective-permute-start.3 = (bf16[128,1452]{1,0:T(8,128)(2,1)S(1)}, bf16[128,1452]{1,0:T(8,128)(2,1)S(1)}, u32[]{:S(2)}, u32[]{:S(2)}) collective-permute-start(bf16[128,1452]{1,0:T(8,128)(2,1)S(1)} %get-tuple-element.18.refs_0_.block_ref), channel_id=1, source_target_pairs={{0,224},{32,0},{64,32},{96,64},{128,96},{160,128},{192,160},{224,1... | collective-permute-start | bytes 1115144 | tf_op jit(solution)/shard_map/ppermute | solution.py:469
  135.1 8.2 %collective-permute-start.4 = (bf16[128,1452]{1,0:T(8,128)(2,1)S(1)}, bf16[128,1452]{1,0:T(8,128)(2,1)S(1)}, u32[]{:S(2)}, u32[]{:S(2)}) collective-permute-start(bf16[128,1452]{1,0:T(8,128)(2,1)S(1)} %collective-permute-done.2.refs_1_.low_ref), channel_id=1, source_target_pairs={{0,32},{32,64},{64,96},{96,128},{128,160},{160,192},{192,224},{224... | collective-permute-start | bytes 1115144 | tf_op jit(solution)/shard_map/ppermute | solution.py:469
  135.1 44.4 %copy-start.9 = (bf16[128,1452]{1,0:T(8,128)(2,1)}, bf16[128,1452]{1,0:T(8,128)(2,1)S(1)}, u32[]{:S(2)}) copy-start(bf16[128,1452]{1,0:T(8,128)(2,1)S(1)} %collective-permute-done.3.refs_2_.high_ref) | copy-start | bytes 1115140
  135.1 23.3 %collective-permute-start.5 = (bf16[128,1452]{1,0:T(8,128)(2,1)S(1)}, bf16[128,1452]{1,0:T(8,128)(2,1)S(1)}, u32[]{:S(2)}, u32[]{:S(2)}) collective-permute-start(bf16[128,1452]{1,0:T(8,128)(2,1)S(1)} %collective-permute-done.3.refs_2_.high_ref), channel_id=1, source_target_pairs={{0,224},{32,0},{64,32},{96,64},{128,96},{160,128},{192,160},{224,1... | collective-permute-start | bytes 1115144 | tf_op jit(solution)/shard_map/ppermute | solution.py:469
  143.3 42.4 %copy-start.11 = (bf16[128,1452]{1,0:T(8,128)(2,1)}, bf16[128,1452]{1,0:T(8,128)(2,1)S(1)}, u32[]{:S(2)}) copy-start(bf16[128,1452]{1,0:T(8,128)(2,1)S(1)} %collective-permute-done.4.refs_0_.low_ref) | copy-start | bytes 1115140
  143.3 17.9 %collective-permute-start.6 = (bf16[128,1452]{1,0:T(8,128)(2,1)S(1)}, bf16[128,1452]{1,0:T(8,128)(2,1)S(1)}, u32[]{:S(2)}, u32[]{:S(2)}) collective-permute-start(bf16[128,1452]{1,0:T(8,128)(2,1)S(1)} %collective-permute-done.4.refs_0_.low_ref), channel_id=1, source_target_pairs={{0,32},{32,64},{64,96},{96,128},{128,160},{160,192},{192,224},{224... | collective-permute-start | bytes 1115144 | tf_op jit(solution)/shard_map/ppermute | solution.py:469
  146.2 34.1 %all-to-all-start = ((bf16[8,48,1440]{2,1,0:T(8,128)(2,1)}), bf16[8,48,1440]{2,1,0:T(8,128)(2,1)S(1)}, u32[]{:S(2)}, u32[]{:S(2)}) async-start(bf16[8,48,1440]{2,1,0:T(8,128)(2,1)} %shard_map.102), calls=%async_computation | async-start | bytes 2359296 | tf_op jit(solution)/shard_map/all_to_all | solution.py:463
  158.4 43.7 %copy-start.13 = (bf16[128,1452]{1,0:T(8,128)(2,1)}, bf16[128,1452]{1,0:T(8,128)(2,1)S(1)}, u32[]{:S(2)}) copy-start(bf16[128,1452]{1,0:T(8,128)(2,1)S(1)} %collective-permute-done.5.refs_1_.high_ref) | copy-start | bytes 1115140
  158.4 11.7 %collective-permute-start.7 = (bf16[128,1452]{1,0:T(8,128)(2,1)S(1)}, bf16[128,1452]{1,0:T(8,128)(2,1)S(1)}, u32[]{:S(2)}, u32[]{:S(2)}) collective-permute-start(bf16[128,1452]{1,0:T(8,128)(2,1)S(1)} %collective-permute-done.5.refs_1_.high_ref), channel_id=1, source_target_pairs={{0,224},{32,0},{64,32},{96,64},{128,96},{160,128},{192,160},{224,1... | collective-permute-start | bytes 1115144 | tf_op jit(solution)/shard_map/ppermute | solution.py:469
  161.3 11.9 %collective-permute-start.8 = (bf16[64,1452]{1,0:T(8,128)(2,1)S(1)}, bf16[64,1452]{1,0:T(8,128)(2,1)S(1)}, u32[]{:S(2)}, u32[]{:S(2)}) collective-permute-start(bf16[64,1452]{1,0:T(8,128)(2,1)S(1)} %slice.53), channel_id=1, source_target_pairs={{0,32},{32,64},{64,96},{96,128},{128,160},{160,192},{192,224},{224... | collective-permute-start | bytes 557576 | tf_op jit(solution)/shard_map/ppermute | solution.py:469
  170.0 7.4 %copy-start.1 = (bf16[128,1452]{1,0:T(8,128)(2,1)}, bf16[128,1452]{1,0:T(8,128)(2,1)S(1)}, u32[]{:S(2)}) copy-start(bf16[128,1452]{1,0:T(8,128)(2,1)S(1)} %collective-permute-done.7.refs_1_.high_ref) | copy-start | bytes 1115140
  170.1 7.3 %collective-permute-start.9 = (bf16[64,1452]{1,0:T(8,128)(2,1)S(1)}, bf16[64,1452]{1,0:T(8,128)(2,1)S(1)}, u32[]{:S(2)}, u32[]{:S(2)}) collective-permute-start(bf16[64,1452]{1,0:T(8,128)(2,1)S(1)} %slice.54), channel_id=1, source_target_pairs={{0,224},{32,0},{64,32},{96,64},{128,96},{160,128},{192,160},{224,1... | collective-permute-start | bytes 557576 | tf_op jit(solution)/shard_map/ppermute | solution.py:469
  180.3 21.8 %all-to-all-start.5 = ((bf16[8,48,1440]{2,1,0:T(8,128)(2,1)}), bf16[8,48,1440]{2,1,0:T(8,128)(2,1)S(1)}, u32[]{:S(2)}, u32[]{:S(2)}) async-start(bf16[8,48,1440]{2,1,0:T(8,128)(2,1)} %shard_map.105), calls=%async_computation.5 | async-start | bytes 2359296 | tf_op jit(solution)/shard_map/all_to_all | solution.py:463
  202.1 16.7 %all-to-all-start.1 = ((bf16[8,32,1440]{2,1,0:T(8,128)(2,1)}), bf16[8,32,1440]{2,1,0:T(8,128)(2,1)S(1)}, u32[]{:S(2)}, u32[]{:S(2)}) async-start(bf16[8,32,1440]{2,1,0:T(8,128)(2,1)} %copy-done), calls=%async_computation.1 | async-start | bytes 1572864 | tf_op jit(solution)/shard_map/all_to_all | solution.py:463
  218.8 25.0 %all-to-all-start.6 = ((bf16[8,48,1440]{2,1,0:T(8,128)(2,1)}), bf16[8,48,1440]{2,1,0:T(8,128)(2,1)S(1)}, u32[]{:S(2)}, u32[]{:S(2)}) async-start(bf16[8,48,1440]{2,1,0:T(8,128)(2,1)} %shard_map.106), calls=%async_computation.6 | async-start | bytes 2359296 | tf_op jit(solution)/shard_map/all_to_all | solution.py:463
  243.8 20.8 %all-to-all-start.4 = ((bf16[8,32,1440]{2,1,0:T(8,128)(2,1)}), bf16[8,32,1440]{2,1,0:T(8,128)(2,1)S(1)}, u32[]{:S(2)}, u32[]{:S(2)}) async-start(bf16[8,32,1440]{2,1,0:T(8,128)(2,1)} %copy-done.16), calls=%async_computation.4 | async-start | bytes 1572864 | tf_op jit(solution)/shard_map/all_to_all | solution.py:463
  249.7 40.9 %copy-start.8 = (bf16[128,1452]{1,0:T(8,128)(2,1)S(1)}, bf16[128,1452]{1,0:T(8,128)(2,1)}, u32[]{:S(2)}) copy-start(bf16[128,1452]{1,0:T(8,128)(2,1)} %copy-done.7) | copy-start | bytes 1115140
  250.2 8.7 %collective-permute-start.10 = (bf16[64,1440]{1,0:T(8,128)(2,1)S(1)}, bf16[64,1440]{1,0:T(8,128)(2,1)S(1)}, u32[]{:S(2)}, u32[]{:S(2)}) collective-permute-start(bf16[64,1440]{1,0:T(8,128)(2,1)S(1)} %get-tuple-element.22), channel_id=1, source_target_pairs={{0,224},{32,0},{64,32},{96,64},{128,96},{160,128},{192,160},{224,1... | collective-permute-start | bytes 552968 | tf_op jit(solution)/shard_map/ppermute | solution.py:469
  253.2 7.4 %collective-permute-start.11 = (bf16[64,1440]{1,0:T(8,128)(2,1)S(1)}, bf16[64,1440]{1,0:T(8,128)(2,1)S(1)}, u32[]{:S(2)}, u32[]{:S(2)}) collective-permute-start(bf16[64,1440]{1,0:T(8,128)(2,1)S(1)} %get-tuple-element.23), channel_id=1, source_target_pairs={{0,32},{32,64},{64,96},{96,128},{128,160},{160,192},{192,224},{224... | collective-permute-start | bytes 552968 | tf_op jit(solution)/shard_map/ppermute | solution.py:469
  261.6 47.5 %copy-start.6 = (bf16[128,1452]{1,0:T(8,128)(2,1)S(1)}, bf16[128,1452]{1,0:T(8,128)(2,1)}, u32[]{:S(2)}) copy-start(bf16[128,1452]{1,0:T(8,128)(2,1)} %copy-done.5) | copy-start | bytes 1115140
  263.1 9.7 %collective-permute-start.12 = (bf16[128,1440]{1,0:T(8,128)(2,1)}, bf16[128,1440]{1,0:T(8,128)(2,1)S(1)}, u32[]{:S(2)}, u32[]{:S(2)}) collective-permute-start(bf16[128,1440]{1,0:T(8,128)(2,1)} %get-tuple-element.24), channel_id=1, source_target_pairs={{0,224},{32,0},{64,32},{96,64},{128,96},{160,128},{192,160},{224,1... | collective-permute-start | bytes 1105928 | tf_op jit(solution)/shard_map/ppermute | solution.py:469
  263.4 10.9 %collective-permute-start.13 = (bf16[128,1440]{1,0:T(8,128)(2,1)}, bf16[128,1440]{1,0:T(8,128)(2,1)S(1)}, u32[]{:S(2)}, u32[]{:S(2)}) collective-permute-start(bf16[128,1440]{1,0:T(8,128)(2,1)} %get-tuple-element.25), channel_id=1, source_target_pairs={{0,32},{32,64},{64,96},{96,128},{128,160},{160,192},{192,224},{224... | collective-permute-start | bytes 1105928 | tf_op jit(solution)/shard_map/ppermute | solution.py:469
  264.6 18.3 %all-to-all-start.3 = ((bf16[8,32,1440]{2,1,0:T(8,128)(2,1)}), bf16[8,32,1440]{2,1,0:T(8,128)(2,1)S(1)}, u32[]{:S(2)}, u32[]{:S(2)}) async-start(bf16[8,32,1440]{2,1,0:T(8,128)(2,1)} %copy-done.15), calls=%async_computation.3 | async-start | bytes 1572864 | tf_op jit(solution)/shard_map/all_to_all | solution.py:463
  277.6 10.1 %collective-permute-start.14 = (bf16[128,1440]{1,0:T(8,128)(2,1)}, bf16[128,1440]{1,0:T(8,128)(2,1)S(1)}, u32[]{:S(2)}, u32[]{:S(2)}) collective-permute-start(bf16[128,1440]{1,0:T(8,128)(2,1)} %get-tuple-element.26), channel_id=1, source_target_pairs={{0,224},{32,0},{64,32},{96,64},{128,96},{160,128},{192,160},{224,1... | collective-permute-start | bytes 1105928 | tf_op jit(solution)/shard_map/ppermute | solution.py:469
  280.7 9.9 %collective-permute-start.15 = (bf16[128,1440]{1,0:T(8,128)(2,1)S(1)}, bf16[128,1440]{1,0:T(8,128)(2,1)S(1)}, u32[]{:S(2)}, u32[]{:S(2)}) collective-permute-start(bf16[128,1440]{1,0:T(8,128)(2,1)S(1)} %get-tuple-element.27), channel_id=1, source_target_pairs={{0,32},{32,64},{64,96},{96,128},{128,160},{160,192},{192,224},{224... | collective-permute-start | bytes 1105928 | tf_op jit(solution)/shard_map/ppermute | solution.py:469
  292.4 16.7 %collective-permute-start.16 = (bf16[128,1440]{1,0:T(8,128)(2,1)S(1)}, bf16[128,1440]{1,0:T(8,128)(2,1)S(1)}, u32[]{:S(2)}, u32[]{:S(2)}) collective-permute-start(bf16[128,1440]{1,0:T(8,128)(2,1)S(1)} %get-tuple-element.28), channel_id=1, source_target_pairs={{0,224},{32,0},{64,32},{96,64},{128,96},{160,128},{192,160},{224,1... | collective-permute-start | bytes 1105928 | tf_op jit(solution)/shard_map/ppermute | solution.py:469
  293.1 16.0 %collective-permute-start.17 = (bf16[128,1440]{1,0:T(8,128)(2,1)S(1)}, bf16[128,1440]{1,0:T(8,128)(2,1)S(1)}, u32[]{:S(2)}, u32[]{:S(2)}) collective-permute-start(bf16[128,1440]{1,0:T(8,128)(2,1)S(1)} %get-tuple-element.29), channel_id=1, source_target_pairs={{0,32},{32,64},{64,96},{96,128},{128,160},{160,192},{192,224},{224... | collective-permute-start | bytes 1105928 | tf_op jit(solution)/shard_map/ppermute | solution.py:469
  (13 other events, 11.7 us)
Sparse Core Ops, SparseCore 0:
  10.1 97.2 all-gather.2
where the time goes:
time: 319 us; the launch traced here: 318 us
  waiting for transfers between devices  151 us (47%)
  starting transfers between devices  63 us (20%)
  Pallas kernels  48.1 us (15%)
  local copies, waits for them, and re-layouts  18.4 us (6%)
  blocking collectives  15.1 us (5%)
  between operations  13.8 us (4%)
  other arithmetic  6.76 us (2%)
    all_gather x1, waiting for transfers between devices, local(): gathered = lax.all_gather(both, SEQ, axis=0)  90.2 us
    ppermute x16, waiting for transfers between devices, pass_on(): return lax.ppermute(rows, 'z', perm)  43 us
    all_to_all x6, starting transfers between devices, plane_exchange(): return lax.all_to_all(rows, PLANE, split_axis=0, concat_axis=0, tiled=True)  37.8 us
    pallas_call x2, Pallas kernels, run_expert(): pl.pallas_call(body, out_shape=[jax.ShapeDtypeStruct(shape, jnp.bfloat16)...  29.9 us
    ppermute x16, starting transfers between devices, pass_on(): return lax.ppermute(rows, 'z', perm)  21.1 us
    all_to_all x6, waiting for transfers between devices, plane_exchange(): return lax.all_to_all(rows, PLANE, split_axis=0, concat_axis=0, tiled=True)  16.9 us
    all_to_all x1, blocking collectives, plane_exchange(): return lax.all_to_all(rows, PLANE, split_axis=0, concat_axis=0, tiled=True)  15.1 us
    unnamed x43, local copies, waits for them, and re-layouts  13.6 us
  transfers between devices with their start and end apart: 25, of which 14 were waited for; matrix products, arithmetic and copies ran while one was open for 4% of the time, Pallas kernels for 12%

commit v1 on v0

--- a/solution.py
+++ b/solution.py
@@ -100,46 +100,43 @@
     return columns == places
 
 
-def select_rows(block, width, first_expert):
-    meta = block[:, width : width + META].astype(jnp.float32)
-    pick = jnp.zeros((block.shape[0], 8 * CAP), jnp.float32)
-    for which in range(TOP):
-        pick = jnp.where(slot_match(meta, first_expert, which), 1.0, pick)
-    return lax.dot_general(
-        pick.astype(jnp.bfloat16),
-        block[:, :width],
-        (((0,), (0,)), ((), ())),
-        preferred_element_type=jnp.float32,
-    ).astype(jnp.bfloat16)
-
-
-def weigh_rows(block, width, first_expert, rows):
-    meta = block[:, width : width + META].astype(jnp.float32)
-    share = jnp.zeros((block.shape[0], 8 * CAP), jnp.float32)
-    for which in range(TOP):
-        share = jnp.where(
-            slot_match(meta, first_expert, which),
-            meta[:, 2 * TOP + which : 2 * TOP + which + 1],
-            share,
-        )
-    return jnp.dot(share.astype(jnp.bfloat16), rows, preferred_element_type=jnp.float32)
-
-
 def dispatch_rows(plane, blocks, width):
     count = len(blocks)
+    tokens = blocks[0].shape[0]
 
     def body(plane_ref, *refs):
-        out_ref = refs[-1]
+        out_ref, share_ref = refs[-2:]
         first_expert = (plane_ref[0] * 8).astype(jnp.float32)
         for number in range(count):
-            rows = select_rows(refs[number][...], width, first_expert)
+            meta = refs[number][:, width : width + META].astype(jnp.float32)
+            pick = jnp.zeros((tokens, 8 * CAP), jnp.float32)
+            share = pick
+            for which in range(TOP):
+                here = slot_match(meta, first_expert, which)
+                pick = jnp.where(here, 1.0, pick)
+                share = jnp.where(here, meta[:, 2 * TOP + which : 2 * TOP + which + 1], share)
+            share_ref[number] = share.astype(jnp.bfloat16)
+            rows = lax.dot_general(
+                pick.astype(jnp.bfloat16),
+                refs[number][:, :width],
+                (((0,), (0,)), ((), ())),
+                preferred_element_type=jnp.float32,
+            ).astype(jnp.bfloat16)
             out_ref[:, number * CAP : (number + 1) * CAP, :] = rows.reshape(8, CAP, width)
 
     return local_call(
         body,
-        jax.ShapeDtypeStruct((8, count * CAP, width), jnp.bfloat16),
+        [
+            jax.ShapeDtypeStruct((8, count * CAP, width), jnp.bfloat16),
+            jax.ShapeDtypeStruct((count, tokens, 8 * CAP), jnp.bfloat16),
+        ],
         [pl.BlockSpec(memory_space=pltpu.SMEM)] + whole(count),
     )(plane, *blocks)
+
+
+def weigh_rows(share, rows):
+    flat = rows.reshape(8 * CAP, rows.shape[-1])
+    return jnp.dot(share, flat, preferred_element_type=jnp.float32)
 
 
 def run_expert(groups, parts, weight_in, weight_out):
@@ -326,32 +323,28 @@
     )(attention, gathered, tokens, gain.reshape(1, width), columns)
 
 
-def combine_far(plane, block, rows, width):
-    half = block.shape[0] // 2
-
-    def body(plane_ref, block_ref, rows_ref, low_ref, high_ref):
-        first_expert = (plane_ref[0] * 8).astype(jnp.float32)
-        summed = weigh_rows(
-            block_ref[...], width, first_expert, rows_ref[:, -CAP:, :].reshape(8 * CAP, width)
-        ).astype(jnp.bfloat16)
-        low_ref[...] = summed[:half]
-        high_ref[...] = summed[half:]
+def combine_far(shares, rows):
+    last, count = shares.shape[0] - 1, shares.shape[1]
+    half, width = count // 2, rows.shape[-1]
+
+    def body(share_ref, rows_ref, low_ref, high_ref):
+        summed = weigh_rows(share_ref[last], rows_ref[:, last * CAP : (last + 1) * CAP, :])
+        low_ref[...] = summed[:half].astype(jnp.bfloat16)
+        high_ref[...] = summed[half:].astype(jnp.bfloat16)
 
     return local_call(
-        body,
-        [jax.ShapeDtypeStruct((half, width), jnp.bfloat16)] * 2,
-        [pl.BlockSpec(memory_space=pltpu.SMEM)] + whole(2),
-    )(plane, block, rows)
-
-
-def combine_pair(plane, blocks, rows, arrived, width):
-    count = blocks[0].shape[0]
-
-    def body(plane_ref, low_ref, high_ref, rows_ref, first_ref, second_ref, *outs):
-        first_expert = (plane_ref[0] * 8).astype(jnp.float32)
-        for number, (block, came) in enumerate(((low_ref, first_ref), (high_ref, second_ref))):
-            part = rows_ref[:, number * CAP : (number + 1) * CAP, :].reshape(8 * CAP, width)
-            summed = weigh_rows(block[...], width, first_expert, part)
+        body, [jax.ShapeDtypeStruct((half, width), jnp.bfloat16)] * 2, whole(2)
+    )(shares, rows)
+
+
+def combine_pair(shares, first, rows, arrived):
+    count, width = shares.shape[1], rows.shape[-1]
+
+    def body(share_ref, rows_ref, rising_ref, falling_ref, *outs):
+        for number, came in enumerate((rising_ref, falling_ref)):
+            summed = weigh_rows(
+                share_ref[first + number], rows_ref[:, number * CAP : (number + 1) * CAP, :]
+            )
             size = came.shape[0]
             if size == count:
                 outs[number][...] = (summed + came[...].astype(jnp.float32)).astype(jnp.bfloat16)
@@ -366,30 +359,22 @@
                 )
 
     return local_call(
-        body,
-        [jax.ShapeDtypeStruct((count, width), jnp.bfloat16)] * 2,
-        [pl.BlockSpec(memory_space=pltpu.SMEM)] + whole(5),
-    )(plane, *blocks, rows, *arrived)
-
-
-def combine_last(plane, block, rows, arrived, residual_mid, width):
-    def body(plane_ref, block_ref, rows_ref, first_ref, second_ref, residual_ref, out_ref):
-        first_expert = (plane_ref[0] * 8).astype(jnp.float32)
-        summed = weigh_rows(
-            block_ref[...], width, first_expert, rows_ref[...].reshape(8 * CAP, width)
-        )
+        body, [jax.ShapeDtypeStruct((count, width), jnp.bfloat16)] * 2, whole(4)
+    )(shares, rows, *arrived)
+
+
+def combine_last(shares, rows, arrived, residual_mid):
+    def body(share_ref, rows_ref, rising_ref, falling_ref, residual_ref, out_ref):
         out_ref[...] = (
             residual_ref[...].astype(jnp.float32)
-            + summed
-            + first_ref[...].astype(jnp.float32)
-            + second_ref[...].astype(jnp.float32)
+            + weigh_rows(share_ref[0], rows_ref[...])
+            + rising_ref[...].astype(jnp.float32)
+            + falling_ref[...].astype(jnp.float32)
         ).astype(jnp.bfloat16)
 
     return local_call(
-        body,
-        jax.ShapeDtypeStruct(residual_mid.shape, jnp.bfloat16),
-        [pl.BlockSpec(memory_space=pltpu.SMEM)] + whole(5),
-    )(plane, block, rows, *arrived, residual_mid)
+        body, jax.ShapeDtypeStruct(residual_mid.shape, jnp.bfloat16), whole(5)
+    )(shares, rows, *arrived, residual_mid)
 
 
 def routing_columns(expert_ids, gate_ints, experts):
@@ -481,9 +466,10 @@
         [rising[2], falling[2]],
         [rising[3], falling[3], far],
     )
-    sent = []
+    sent, shares = [], []
     for group in picked:
-        rows = dispatch_rows(plane, group, width)
+        rows, share = dispatch_rows(plane, group, width)
+        shares.append(share)
         sent.append(plane_exchange(rows))
     made_0, made_1, made_2 = run_expert(
         sent[:2], ((CAP, 2 * CAP), (2 * CAP,)), weight_in, weight_out
@@ -491,20 +477,16 @@
     (made_3,) = run_expert(sent[2:], ((3 * CAP,),), weight_in, weight_out)
     back = [plane_exchange(rows) for rows in (made_0, made_1, made_2, made_3)]
 
-    to_rising, to_falling = combine_far(plane, far, back[3], width)
+    to_rising, to_falling = combine_far(shares[2], back[3])
     for step in (3, 2, 1):
         to_rising = pass_on(to_rising, backward)
         to_falling = pass_on(to_falling, forward)
         to_rising, to_falling = combine_pair(
-            plane,
-            (rising[step], falling[step]),
-            back[step],
-            (to_rising, to_falling),
-            width,
+            shares[step - 1], int(step == 1), back[step], (to_rising, to_falling)
         )
     to_rising = pass_on(to_rising, backward)
     to_falling = pass_on(to_falling, forward)
-    return combine_last(plane, own, back[0], (to_rising, to_falling), residual_mid, width)
+    return combine_last(shares[0], back[0], (to_rising, to_falling), residual_mid)
 
 
 def solution(mesh):

time: 319 us -> 299 us (0.937)
  local copies, waits for them, and re-layouts: 18.4 us -> 11 us
  starting transfers between devices: 63 us -> 56.6 us
  waiting for transfers between devices: 151 us -> 146 us
    ppermute x16, waiting for transfers between devices: 43 us -> 32.3 us  [pass_on(): return lax.ppermute(rows, 'z', perm)]
    unnamed x43 -> x14, local copies, waits for them, and re-layouts: 13.6 us -> 6.18 us
    all_to_all x6, waiting for transfers between devices: 16.9 us -> 22.3 us  [plane_exchange(): return lax.all_to_all(rows, PLANE, split_axis=0, concat_axis=0, tiled=True)]
    ppermute x16, starting transfers between devices: 21.1 us -> 15.9 us  [pass_on(): return lax.ppermute(rows, 'z', perm)]
  transfers between devices with their start and end apart: 25 -> 25, of which waited for: 14 -> 15; matrix products, arithmetic and copies ran while one was open for 4% -> 4% of each run, Pallas kernels for 12% -> 13%
where the time goes in v1:
time: 299 us; the launch traced here: 298 us
  waiting for transfers between devices  146 us (49%)
  starting transfers between devices  56.6 us (19%)
  Pallas kernels  46.8 us (16%)
  blocking collectives  15.2 us (5%)
  between operations  13.8 us (5%)
  local copies, waits for them, and re-layouts  11 us (4%)
  other arithmetic  6.79 us (2%)
    all_gather x1, waiting for transfers between devices, local(): gathered = lax.all_gather(both, SEQ, axis=0)  90.2 us
    all_to_all x6, starting transfers between devices, plane_exchange(): return lax.all_to_all(rows, PLANE, split_axis=0, concat_axis=0, tiled=True)  36.5 us
    ppermute x16, waiting for transfers between devices, pass_on(): return lax.ppermute(rows, 'z', perm)  32.3 us
    pallas_call x2, Pallas kernels, run_expert(): pl.pallas_call(body, out_shape=[jax.ShapeDtypeStruct(shape, jnp.bfloat16)...  30.7 us
    all_to_all x6, waiting for transfers between devices, plane_exchange(): return lax.all_to_all(rows, PLANE, split_axis=0, concat_axis=0, tiled=True)  22.3 us
    ppermute x16, starting transfers between devices, pass_on(): return lax.ppermute(rows, 'z', perm)  15.9 us
    all_to_all x1, blocking collectives, plane_exchange(): return lax.all_to_all(rows, PLANE, split_axis=0, concat_axis=0, tiled=True)  15.2 us
    unnamed x14, local copies, waits for them, and re-layouts  6.18 us
  transfers between devices with their start and end apart: 25, of which 15 were waited for; matrix products, arithmetic and copies ran while one was open for 4% of the time, Pallas kernels for 13%

profile of v1, /device:TPU:1, one launch (start us, length us, event | category | flops | bytes accessed | tf_op | source)
XLA Modules:
  0.0 298.0 jit_solution(17369147701785883052)
XLA Ops:
  6.5 1.7 pad_maximum_fusion.1
  17.1 90.2 %all-gather.3.cloned.1.call-done = bf16[4608,1440]{1,0:T(8,128)(2,1)} async-done(((bf16[72,1440]{1,0:T(8,128)(2,1)}), bf16[4608,1440]{1,0:T(8,128)(2,1)}) %all-gather.3.cloned.1.call-update) | async-done | bytes 13271056 | tf_op jit(solution)/shard_map/all_gather | solution.py:414
  107.3 5.0 %shard_map.100 = f32[128,2560]{1,0:T(8,128)S(1)} custom-call(bf16[128,1440]{1,0:T(8,128)(2,1)S(1)} %copy.71.tokens_ref, f32[1,1440]{1,0:T(1,128)S(1)} %reshape.176.gain_ref, bf16[64,72,1440]{2,1,0:T(8,128)(2,1)} %bitcast.53), custom_call_target="tpu_custom_call" | custom-call | tf_op jit(solution)/shard_map/pallas_call | solution.py:266
  112.6 2.0 collective-permute-start
  115.1 2.1 collective-permute-start.1
  121.8 3.4 %shard_map.101 = (bf16[128,1440]{1,0:T(8,128)(2,1)S(1)}, bf16[128,1452]{1,0:T(8,128)(2,1)S(1)}) custom-call(bf16[128,2048]{1,0:T(8,128)(2,1)S(1)} %copy.82.attention_ref, bf16[64,72,1440]{2,1,0:T(8,128)(2,1)} %bitcast.54, bf16[128,1440]{1,0:T(8,128)(2,1)S(1)} %copy.71.tokens_ref, f32[1,1440]{1,0:T(1,128)S(1)} %reshape.179.gain_ref, ...), custom_call_target="tpu_custom_call" | custom-call | tf_op jit(solution)/shard_map/pallas_call | solution.py:310
  127.5 5.6 %collective-permute-done.3.refs_2_ = bf16[128,1452]{1,0:T(8,128)(2,1)S(1)} collective-permute-done((bf16[128,1452]{1,0:T(8,128)(2,1)S(1)}, bf16[128,1452]{1,0:T(8,128)(2,1)S(1)}, u32[]{:S(2)}, u32[]{:S(2)}) %collective-permute-start.3) | collective-permute-done | bytes 371744 | tf_op jit(solution)/shard_map/ppermute | solution.py:454
  133.1 1.9 collective-permute-start.5
  134.9 2.0 shard_map.102
  136.9 11.3 %all-to-all-start = ((bf16[8,48,1440]{2,1,0:T(8,128)(2,1)}), bf16[8,48,1440]{2,1,0:T(8,128)(2,1)S(1)}, u32[]{:S(2)}, u32[]{:S(2)}) async-start(bf16[8,48,1440]{2,1,0:T(8,128)(2,1)} %get-tuple-element.26), calls=%async_computation | async-start | bytes 2359296 | tf_op jit(solution)/shard_map/all_to_all | solution.py:448
  148.2 3.0 collective-permute-start.7
  151.1 8.1 %collective-permute-done.7.refs_1_ = bf16[128,1452]{1,0:T(8,128)(2,1)S(1)} collective-permute-done((bf16[128,1452]{1,0:T(8,128)(2,1)S(1)}, bf16[128,1452]{1,0:T(8,128)(2,1)S(1)}, u32[]{:S(2)}, u32[]{:S(2)}) %collective-permute-start.7) | collective-permute-done | bytes 371744 | tf_op jit(solution)/shard_map/ppermute | solution.py:454
  159.3 3.5 %collective-permute-start.9 = (bf16[64,1452]{1,0:T(8,128)(2,1)S(1)}, bf16[64,1452]{1,0:T(8,128)(2,1)S(1)}, u32[]{:S(2)}, u32[]{:S(2)}) collective-permute-start(bf16[64,1452]{1,0:T(8,128)(2,1)S(1)} %slice.54), channel_id=1, source_target_pairs={{0,224},{32,0},{64,32},{96,64},{128,96},{160,128},{192,160},{224,1... | collective-permute-start | bytes 557576 | tf_op jit(solution)/shard_map/ppermute | solution.py:454
  162.9 2.9 collective-permute-done.9
  165.8 3.2 %collective-permute-done.8 = bf16[64,1452]{1,0:T(8,128)(2,1)S(1)} collective-permute-done((bf16[64,1452]{1,0:T(8,128)(2,1)S(1)}, bf16[64,1452]{1,0:T(8,128)(2,1)S(1)}, u32[]{:S(2)}, u32[]{:S(2)}) %collective-permute-start.8) | collective-permute-done | bytes 185888 | tf_op jit(solution)/shard_map/ppermute | solution.py:454
  169.0 1.9 shard_map.105
  171.0 6.8 %all-to-all-start.5 = ((bf16[8,48,1440]{2,1,0:T(8,128)(2,1)}), bf16[8,48,1440]{2,1,0:T(8,128)(2,1)S(1)}, u32[]{:S(2)}, u32[]{:S(2)}) async-start(bf16[8,48,1440]{2,1,0:T(8,128)(2,1)} %get-tuple-element.33), calls=%async_computation.5 | async-start | bytes 2359296 | tf_op jit(solution)/shard_map/all_to_all | solution.py:448
  179.4 14.8 %all-to-all-done.5.refs_0_ = bf16[8,48,1440]{2,1,0:T(8,128)(2,1)S(1)} async-done(((bf16[8,48,1440]{2,1,0:T(8,128)(2,1)}), bf16[8,48,1440]{2,1,0:T(8,128)(2,1)S(1)}, u32[]{:S(2)}, u32[]{:S(2)}) %all-to-all-start.5) | async-done | bytes 1105952 | tf_op jit(solution)/shard_map/all_to_all | solution.py:448
  194.1 4.4 %all-to-all-start.1 = ((bf16[8,32,1440]{2,1,0:T(8,128)(2,1)}), bf16[8,32,1440]{2,1,0:T(8,128)(2,1)S(1)}, u32[]{:S(2)}, u32[]{:S(2)}) async-start(bf16[8,32,1440]{2,1,0:T(8,128)(2,1)} %copy-done.1), calls=%async_computation.1 | async-start | bytes 1572864 | tf_op jit(solution)/shard_map/all_to_all | solution.py:448
  198.6 12.2 %shard_map.106 = bf16[8,48,1440]{2,1,0:T(8,128)(2,1)} custom-call(bf16[8,48,1440]{2,1,0:T(8,128)(2,1)S(1)} %all-to-all-done.5.refs_0_, bf16[1,1440,2880]{2,1,0:T(8,128)(2,1)} %refs_1_.1, bf16[1,1440,1440]{2,1,0:T(8,128)(2,1)} %refs_2_.3), custom_call_target="tpu_custom_call" | custom-call | tf_op jit(solution)/shard_map/pallas_call | solution.py:225
  210.8 4.8 %all-to-all-start.6 = ((bf16[8,48,1440]{2,1,0:T(8,128)(2,1)}), bf16[8,48,1440]{2,1,0:T(8,128)(2,1)S(1)}, u32[]{:S(2)}, u32[]{:S(2)}) async-start(bf16[8,48,1440]{2,1,0:T(8,128)(2,1)} %shard_map.106), calls=%async_computation.6 | async-start | bytes 2359296 | tf_op jit(solution)/shard_map/all_to_all | solution.py:448
  215.7 18.4 %shard_map.104 = (bf16[8,16,1440]{2,1,0:T(8,128)(2,1)S(1)}, bf16[8,32,1440]{2,1,0:T(8,128)(2,1)}, bf16[8,32,1440]{2,1,0:T(8,128)(2,1)S(1)}) custom-call(bf16[8,48,1440]{2,1,0:T(8,128)(2,1)S(1)} %all-to-all-done.refs_0_, bf16[8,32,1440]{2,1,0:T(8,128)(2,1)S(1)} %all-to-all-done.1.refs_1_, bf16[1,1440,2880]{2,1,0:T(8,128)(2,1)} %refs_1_.1, ...), custom_call_target="tpu_custom_call" | custom-call | tf_op jit(solution)/shard_map/pallas_call | solution.py:225
  235.7 4.8 %all-to-all-start.4 = ((bf16[8,32,1440]{2,1,0:T(8,128)(2,1)}), bf16[8,32,1440]{2,1,0:T(8,128)(2,1)S(1)}, u32[]{:S(2)}, u32[]{:S(2)}) async-start(bf16[8,32,1440]{2,1,0:T(8,128)(2,1)} %copy-done), calls=%async_computation.4 | async-start | bytes 1572864 | tf_op jit(solution)/shard_map/all_to_all | solution.py:448
  240.9 1.5 collective-permute-start.11
  242.4 5.0 %collective-permute-done.10.rising_ref = bf16[64,1440]{1,0:T(8,128)(2,1)S(1)} collective-permute-done((bf16[64,1440]{1,0:T(8,128)(2,1)S(1)}, bf16[64,1440]{1,0:T(8,128)(2,1)S(1)}, u32[]{:S(2)}, u32[]{:S(2)}) %collective-permute-start.10) | collective-permute-done | bytes 184352 | tf_op jit(solution)/shard_map/ppermute | solution.py:454
  249.8 1.3 collective-permute-start.13
  251.2 1.6 all-to-all-done.4.rows_ref
  252.7 4.4 %all-to-all-start.3 = ((bf16[8,32,1440]{2,1,0:T(8,128)(2,1)}), bf16[8,32,1440]{2,1,0:T(8,128)(2,1)S(1)}, u32[]{:S(2)}, u32[]{:S(2)}) async-start(bf16[8,32,1440]{2,1,0:T(8,128)(2,1)} %get-tuple-element.29), calls=%async_computation.3 | async-start | bytes 1572864 | tf_op jit(solution)/shard_map/all_to_all | solution.py:448
  257.1 2.5 collective-permute-done.12.rising_ref
  263.3 6.0 %all-to-all-done.3.rows_ref = bf16[8,32,1440]{2,1,0:T(8,128)(2,1)S(1)} async-done(((bf16[8,32,1440]{2,1,0:T(8,128)(2,1)}), bf16[8,32,1440]{2,1,0:T(8,128)(2,1)S(1)}, u32[]{:S(2)}, u32[]{:S(2)}) %all-to-all-start.3) | async-done | bytes 737312 | tf_op jit(solution)/shard_map/all_to_all | solution.py:448
  269.3 1.5 collective-permute-done.14.rising_ref
  273.7 15.2 %all_to_all.35.rows_ref = bf16[8,16,1440]{2,1,0:T(8,128)(2,1)S(1)} all-to-all(bf16[8,16,1440]{2,1,0:T(8,128)(2,1)S(1)} %copy-done.3), channel_id=1, replica_groups=mesh['z'=8,'y'=4,'c'=2,'x'=4] {'y','c'}, dimensions={0} | all-to-all | bytes 737280 | tf_op jit(solution)/shard_map/all_to_all | solution.py:448
  (92 shorter events, 31.2 us)
Async XLA Ops:
  6.5 100.8 %all-gather.3.cloned.1.call-start = ((), (), s32[]{:S(2)}) async-start(), calls=%async_computation.7 | async-start | bytes 14376960 | tf_op jit(solution)/shard_map/all_gather | solution.py:414
  112.6 7.8 %collective-permute-start = (bf16[128,4,64]{0,2,1:T(8,128)(2,1)S(1)}, bf16[128,4,64]{0,2,1:T(8,128)(2,1)S(1)}, u32[]{:S(2)}, u32[]{:S(2)}) collective-permute-start(bf16[128,4,64]{0,2,1:T(8,128)(2,1)S(1)} %bitcast.61), channel_id=1, source_target_pairs={{0,4},{4,8},{8,12},{12,16},{16,20},{20,24},{24,28},{28,32},{32,36}... | collective-permute-start | bytes 196616 | tf_op jit(solution)/shard_map/ppermute | solution.py:33
  115.1 3.5 %collective-permute-start.1 = (bf16[128,4,64]{0,2,1:T(8,128)(2,1)S(1)}, bf16[128,4,64]{0,2,1:T(8,128)(2,1)S(1)}, u32[]{:S(2)}, u32[]{:S(2)}) collective-permute-start(bf16[128,4,64]{0,2,1:T(8,128)(2,1)S(1)} %pad_maximum_fusion.2), channel_id=1, source_target_pairs={{0,4},{4,8},{8,12},{12,16},{16,20},{20,24},{24,28},{28,32},{32,36}... | collective-permute-start | bytes 196616 | tf_op jit(solution)/shard_map/ppermute | solution.py:33
  125.2 0.8 copy-start.4
  126.0 7.1 %collective-permute-start.3 = (bf16[128,1452]{1,0:T(8,128)(2,1)S(1)}, bf16[128,1452]{1,0:T(8,128)(2,1)S(1)}, u32[]{:S(2)}, u32[]{:S(2)}) collective-permute-start(bf16[128,1452]{1,0:T(8,128)(2,1)S(1)} %get-tuple-element.24.refs_0_), channel_id=1, source_target_pairs={{0,224},{32,0},{64,32},{96,64},{128,96},{160,128},{192,160},{224,1... | collective-permute-start | bytes 1115144 | tf_op jit(solution)/shard_map/ppermute | solution.py:454
  127.1 7.8 %collective-permute-start.2 = (bf16[128,1452]{1,0:T(8,128)(2,1)S(1)}, bf16[128,1452]{1,0:T(8,128)(2,1)S(1)}, u32[]{:S(2)}, u32[]{:S(2)}) collective-permute-start(bf16[128,1452]{1,0:T(8,128)(2,1)S(1)} %get-tuple-element.24.refs_0_), channel_id=1, source_target_pairs={{0,32},{32,64},{64,96},{96,128},{128,160},{160,192},{192,224},{224... | collective-permute-start | bytes 1115144 | tf_op jit(solution)/shard_map/ppermute | solution.py:454
  133.1 15.1 %collective-permute-start.5 = (bf16[128,1452]{1,0:T(8,128)(2,1)S(1)}, bf16[128,1452]{1,0:T(8,128)(2,1)S(1)}, u32[]{:S(2)}, u32[]{:S(2)}) collective-permute-start(bf16[128,1452]{1,0:T(8,128)(2,1)S(1)} %collective-permute-done.3.refs_2_), channel_id=1, source_target_pairs={{0,224},{32,0},{64,32},{96,64},{128,96},{160,128},{192,160},{224,1... | collective-permute-start | bytes 1115144 | tf_op jit(solution)/shard_map/ppermute | solution.py:454
  134.9 16.2 %collective-permute-start.4 = (bf16[128,1452]{1,0:T(8,128)(2,1)S(1)}, bf16[128,1452]{1,0:T(8,128)(2,1)S(1)}, u32[]{:S(2)}, u32[]{:S(2)}) collective-permute-start(bf16[128,1452]{1,0:T(8,128)(2,1)S(1)} %collective-permute-done.2.refs_1_), channel_id=1, source_target_pairs={{0,32},{32,64},{64,96},{96,128},{128,160},{160,192},{192,224},{224... | collective-permute-start | bytes 1115144 | tf_op jit(solution)/shard_map/ppermute | solution.py:454
  136.9 34.1 %all-to-all-start = ((bf16[8,48,1440]{2,1,0:T(8,128)(2,1)}), bf16[8,48,1440]{2,1,0:T(8,128)(2,1)S(1)}, u32[]{:S(2)}, u32[]{:S(2)}) async-start(bf16[8,48,1440]{2,1,0:T(8,128)(2,1)} %get-tuple-element.26), calls=%async_computation | async-start | bytes 2359296 | tf_op jit(solution)/shard_map/all_to_all | solution.py:448
  148.2 11.1 %collective-permute-start.7 = (bf16[128,1452]{1,0:T(8,128)(2,1)S(1)}, bf16[128,1452]{1,0:T(8,128)(2,1)S(1)}, u32[]{:S(2)}, u32[]{:S(2)}) collective-permute-start(bf16[128,1452]{1,0:T(8,128)(2,1)S(1)} %collective-permute-done.5.refs_1_), channel_id=1, source_target_pairs={{0,224},{32,0},{64,32},{96,64},{128,96},{160,128},{192,160},{224,1... | collective-permute-start | bytes 1115144 | tf_op jit(solution)/shard_map/ppermute | solution.py:454
  151.1 11.6 %collective-permute-start.6 = (bf16[128,1452]{1,0:T(8,128)(2,1)S(1)}, bf16[128,1452]{1,0:T(8,128)(2,1)S(1)}, u32[]{:S(2)}, u32[]{:S(2)}) collective-permute-start(bf16[128,1452]{1,0:T(8,128)(2,1)S(1)} %collective-permute-done.4.refs_0_), channel_id=1, source_target_pairs={{0,32},{32,64},{64,96},{96,128},{128,160},{160,192},{192,224},{224... | collective-permute-start | bytes 1115144 | tf_op jit(solution)/shard_map/ppermute | solution.py:454
  159.3 6.5 %collective-permute-start.9 = (bf16[64,1452]{1,0:T(8,128)(2,1)S(1)}, bf16[64,1452]{1,0:T(8,128)(2,1)S(1)}, u32[]{:S(2)}, u32[]{:S(2)}) collective-permute-start(bf16[64,1452]{1,0:T(8,128)(2,1)S(1)} %slice.54), channel_id=1, source_target_pairs={{0,224},{32,0},{64,32},{96,64},{128,96},{160,128},{192,160},{224,1... | collective-permute-start | bytes 557576 | tf_op jit(solution)/shard_map/ppermute | solution.py:454
  162.8 6.2 %collective-permute-start.8 = (bf16[64,1452]{1,0:T(8,128)(2,1)S(1)}, bf16[64,1452]{1,0:T(8,128)(2,1)S(1)}, u32[]{:S(2)}, u32[]{:S(2)}) collective-permute-start(bf16[64,1452]{1,0:T(8,128)(2,1)S(1)} %slice.53), channel_id=1, source_target_pairs={{0,32},{32,64},{64,96},{96,128},{128,160},{160,192},{192,224},{224... | collective-permute-start | bytes 557576 | tf_op jit(solution)/shard_map/ppermute | solution.py:454
  171.0 23.2 %all-to-all-start.5 = ((bf16[8,48,1440]{2,1,0:T(8,128)(2,1)}), bf16[8,48,1440]{2,1,0:T(8,128)(2,1)S(1)}, u32[]{:S(2)}, u32[]{:S(2)}) async-start(bf16[8,48,1440]{2,1,0:T(8,128)(2,1)} %get-tuple-element.33), calls=%async_computation.5 | async-start | bytes 2359296 | tf_op jit(solution)/shard_map/all_to_all | solution.py:448
  178.5 0.9 copy-start.1
  194.1 16.7 %all-to-all-start.1 = ((bf16[8,32,1440]{2,1,0:T(8,128)(2,1)}), bf16[8,32,1440]{2,1,0:T(8,128)(2,1)S(1)}, u32[]{:S(2)}, u32[]{:S(2)}) async-start(bf16[8,32,1440]{2,1,0:T(8,128)(2,1)} %copy-done.1), calls=%async_computation.1 | async-start | bytes 1572864 | tf_op jit(solution)/shard_map/all_to_all | solution.py:448
  210.8 24.9 %all-to-all-start.6 = ((bf16[8,48,1440]{2,1,0:T(8,128)(2,1)}), bf16[8,48,1440]{2,1,0:T(8,128)(2,1)S(1)}, u32[]{:S(2)}, u32[]{:S(2)}) async-start(bf16[8,48,1440]{2,1,0:T(8,128)(2,1)} %shard_map.106), calls=%async_computation.6 | async-start | bytes 2359296 | tf_op jit(solution)/shard_map/all_to_all | solution.py:448
  234.1 0.9 copy-start
  235.0 0.7 copy-start.2
  235.7 17.0 %all-to-all-start.4 = ((bf16[8,32,1440]{2,1,0:T(8,128)(2,1)}), bf16[8,32,1440]{2,1,0:T(8,128)(2,1)S(1)}, u32[]{:S(2)}, u32[]{:S(2)}) async-start(bf16[8,32,1440]{2,1,0:T(8,128)(2,1)} %copy-done), calls=%async_computation.4 | async-start | bytes 1572864 | tf_op jit(solution)/shard_map/all_to_all | solution.py:448
  240.6 33.2 %copy-start.3 = (bf16[8,16,1440]{2,1,0:T(8,128)(2,1)S(1)}, bf16[8,16,1440]{2,1,0:T(8,128)(2,1)}, u32[]{:S(2)}) copy-start(bf16[8,16,1440]{2,1,0:T(8,128)(2,1)} %copy-done.2) | copy-start | bytes 1105924
  240.8 6.5 %collective-permute-start.10 = (bf16[64,1440]{1,0:T(8,128)(2,1)S(1)}, bf16[64,1440]{1,0:T(8,128)(2,1)S(1)}, u32[]{:S(2)}, u32[]{:S(2)}) collective-permute-start(bf16[64,1440]{1,0:T(8,128)(2,1)S(1)} %get-tuple-element.34), channel_id=1, source_target_pairs={{0,224},{32,0},{64,32},{96,64},{128,96},{160,128},{192,160},{224,1... | collective-permute-start | bytes 552968 | tf_op jit(solution)/shard_map/ppermute | solution.py:454
  240.9 7.6 %collective-permute-start.11 = (bf16[64,1440]{1,0:T(8,128)(2,1)S(1)}, bf16[64,1440]{1,0:T(8,128)(2,1)S(1)}, u32[]{:S(2)}, u32[]{:S(2)}) collective-permute-start(bf16[64,1440]{1,0:T(8,128)(2,1)S(1)} %get-tuple-element.35), channel_id=1, source_target_pairs={{0,32},{32,64},{64,96},{96,128},{128,160},{160,192},{192,224},{224... | collective-permute-start | bytes 552968 | tf_op jit(solution)/shard_map/ppermute | solution.py:454
  249.7 9.9 %collective-permute-start.12 = (bf16[128,1440]{1,0:T(8,128)(2,1)}, bf16[128,1440]{1,0:T(8,128)(2,1)S(1)}, u32[]{:S(2)}, u32[]{:S(2)}) collective-permute-start(bf16[128,1440]{1,0:T(8,128)(2,1)} %get-tuple-element.36), channel_id=1, source_target_pairs={{0,224},{32,0},{64,32},{96,64},{128,96},{160,128},{192,160},{224,1... | collective-permute-start | bytes 1105928 | tf_op jit(solution)/shard_map/ppermute | solution.py:454
  249.8 11.1 %collective-permute-start.13 = (bf16[128,1440]{1,0:T(8,128)(2,1)}, bf16[128,1440]{1,0:T(8,128)(2,1)S(1)}, u32[]{:S(2)}, u32[]{:S(2)}) collective-permute-start(bf16[128,1440]{1,0:T(8,128)(2,1)} %get-tuple-element.37), channel_id=1, source_target_pairs={{0,32},{32,64},{64,96},{96,128},{128,160},{160,192},{192,224},{224... | collective-permute-start | bytes 1105928 | tf_op jit(solution)/shard_map/ppermute | solution.py:454
  252.7 16.6 %all-to-all-start.3 = ((bf16[8,32,1440]{2,1,0:T(8,128)(2,1)}), bf16[8,32,1440]{2,1,0:T(8,128)(2,1)S(1)}, u32[]{:S(2)}, u32[]{:S(2)}) async-start(bf16[8,32,1440]{2,1,0:T(8,128)(2,1)} %get-tuple-element.29), calls=%async_computation.3 | async-start | bytes 1572864 | tf_op jit(solution)/shard_map/all_to_all | solution.py:448
  261.9 9.0 %collective-permute-start.14 = (bf16[128,1440]{1,0:T(8,128)(2,1)}, bf16[128,1440]{1,0:T(8,128)(2,1)S(1)}, u32[]{:S(2)}, u32[]{:S(2)}) collective-permute-start(bf16[128,1440]{1,0:T(8,128)(2,1)} %get-tuple-element.38), channel_id=1, source_target_pairs={{0,224},{32,0},{64,32},{96,64},{128,96},{160,128},{192,160},{224,1... | collective-permute-start | bytes 1105928 | tf_op jit(solution)/shard_map/ppermute | solution.py:454
  262.2 9.6 %collective-permute-start.15 = (bf16[128,1440]{1,0:T(8,128)(2,1)S(1)}, bf16[128,1440]{1,0:T(8,128)(2,1)S(1)}, u32[]{:S(2)}, u32[]{:S(2)}) collective-permute-start(bf16[128,1440]{1,0:T(8,128)(2,1)S(1)} %get-tuple-element.39), channel_id=1, source_target_pairs={{0,32},{32,64},{64,96},{96,128},{128,160},{160,192},{192,224},{224... | collective-permute-start | bytes 1105928 | tf_op jit(solution)/shard_map/ppermute | solution.py:454
  272.2 16.7 %collective-permute-start.16 = (bf16[128,1440]{1,0:T(8,128)(2,1)S(1)}, bf16[128,1440]{1,0:T(8,128)(2,1)S(1)}, u32[]{:S(2)}, u32[]{:S(2)}) collective-permute-start(bf16[128,1440]{1,0:T(8,128)(2,1)S(1)} %get-tuple-element.40), channel_id=1, source_target_pairs={{0,224},{32,0},{64,32},{96,64},{128,96},{160,128},{192,160},{224,1... | collective-permute-start | bytes 1105928 | tf_op jit(solution)/shard_map/ppermute | solution.py:454
  272.7 16.2 %collective-permute-start.17 = (bf16[128,1440]{1,0:T(8,128)(2,1)S(1)}, bf16[128,1440]{1,0:T(8,128)(2,1)S(1)}, u32[]{:S(2)}, u32[]{:S(2)}) collective-permute-start(bf16[128,1440]{1,0:T(8,128)(2,1)S(1)} %get-tuple-element.41), channel_id=1, source_target_pairs={{0,32},{32,64},{64,96},{96,128},{128,160},{160,192},{192,224},{224... | collective-permute-start | bytes 1105928 | tf_op jit(solution)/shard_map/ppermute | solution.py:454
  288.9 1.0 copy-start.5
Sparse Core Ops, SparseCore 0:
  10.1 97.2 all-gather.2

commit v2 on v1

--- a/solution.py
+++ b/solution.py
@@ -337,13 +337,13 @@
     )(shares, rows)
 
 
-def combine_pair(shares, first, rows, arrived):
+def combine_pair(shares, rows, arrived):
     count, width = shares.shape[1], rows.shape[-1]
 
     def body(share_ref, rows_ref, rising_ref, falling_ref, *outs):
         for number, came in enumerate((rising_ref, falling_ref)):
             summed = weigh_rows(
-                share_ref[first + number], rows_ref[:, number * CAP : (number + 1) * CAP, :]
+                share_ref[number], rows_ref[:, number * CAP : (number + 1) * CAP, :]
             )
             size = came.shape[0]
             if size == count:
@@ -462,7 +462,8 @@
         axis=0,
     )
     picked = (
-        [own, rising[1], falling[1]],
+        [own],
+        [rising[1], falling[1]],
         [rising[2], falling[2]],
         [rising[3], falling[3], far],
     )
@@ -472,17 +473,17 @@
         shares.append(share)
         sent.append(plane_exchange(rows))
     made_0, made_1, made_2 = run_expert(
-        sent[:2], ((CAP, 2 * CAP), (2 * CAP,)), weight_in, weight_out
-    )
-    (made_3,) = run_expert(sent[2:], ((3 * CAP,),), weight_in, weight_out)
+        sent[:3], ((CAP,), (2 * CAP,), (2 * CAP,)), weight_in, weight_out
+    )
+    (made_3,) = run_expert(sent[3:], ((3 * CAP,),), weight_in, weight_out)
     back = [plane_exchange(rows) for rows in (made_0, made_1, made_2, made_3)]
 
-    to_rising, to_falling = combine_far(shares[2], back[3])
+    to_rising, to_falling = combine_far(shares[3], back[3])
     for step in (3, 2, 1):
         to_rising = pass_on(to_rising, backward)
         to_falling = pass_on(to_falling, forward)
         to_rising, to_falling = combine_pair(
-            shares[step - 1], int(step == 1), back[step], (to_rising, to_falling)
+            shares[step], back[step], (to_rising, to_falling)
         )
     to_rising = pass_on(to_rising, backward)
     to_falling = pass_on(to_falling, forward)

time: 299 us -> 300 us (level)
  starting transfers between devices: 56.6 us -> 61.4 us
  waiting for transfers between devices: 146 us -> 142 us
    ppermute x16, waiting for transfers between devices: 32.3 us -> 26.5 us  [pass_on(): return lax.ppermute(rows, 'z', perm)]
    all_to_all x6 -> x7, starting transfers between devices: 36.5 us -> 41.7 us  [plane_exchange(): return lax.all_to_all(rows, PLANE, split_axis=0, concat_axis=0, tiled=True)]
    all_to_all x6 -> x7, waiting for transfers between devices: 22.3 us -> 23.6 us  [plane_exchange(): return lax.all_to_all(rows, PLANE, split_axis=0, concat_axis=0, tiled=True)]
    unnamed x14 -> x22, local copies, waits for them, and re-layouts: 6.18 us -> 5.73 us
  transfers between devices with their start and end apart: 25 -> 26, of which waited for: 15 -> 15; matrix products, arithmetic and copies ran while one was open for 4% -> 4% of each run, Pallas kernels for 13% -> 13%
where the time goes in v2:
time: 300 us; the launch traced here: 299 us
  waiting for transfers between devices  142 us (47%)
  starting transfers between devices  61.4 us (20%)
  Pallas kernels  47.8 us (16%)
  blocking collectives  15 us (5%)
  between operations  13.8 us (5%)
  local copies, waits for them, and re-layouts  10.5 us (4%)
  other arithmetic  6.8 us (2%)
    all_gather x1, waiting for transfers between devices, local(): gathered = lax.all_gather(both, SEQ, axis=0)  90.2 us
    all_to_all x7, starting transfers between devices, plane_exchange(): return lax.all_to_all(rows, PLANE, split_axis=0, concat_axis=0, tiled=True)  41.7 us
    pallas_call x2, Pallas kernels, run_expert(): pl.pallas_call(body, out_shape=[jax.ShapeDtypeStruct(shape, jnp.bfloat16)...  30.6 us
    ppermute x16, waiting for transfers between devices, pass_on(): return lax.ppermute(rows, 'z', perm)  26.5 us
    all_to_all x7, waiting for transfers between devices, plane_exchange(): return lax.all_to_all(rows, PLANE, split_axis=0, concat_axis=0, tiled=True)  23.6 us
    ppermute x16, starting transfers between devices, pass_on(): return lax.ppermute(rows, 'z', perm)  15.5 us
    all_to_all x1, blocking collectives, plane_exchange(): return lax.all_to_all(rows, PLANE, split_axis=0, concat_axis=0, tiled=True)  15 us
  transfers between devices with their start and end apart: 26, of which 15 were waited for; matrix products, arithmetic and copies ran while one was open for 4% of the time, Pallas kernels for 13%

profile of v2, /device:TPU:1, one launch (start us, length us, event | category | flops | bytes accessed | tf_op | source)
XLA Modules:
  0.0 298.8 jit_solution(5249938041487122567)
XLA Ops:
  6.5 1.7 pad_maximum_fusion.1
  17.1 90.2 %all-gather.3.cloned.1.call-done = bf16[4608,1440]{1,0:T(8,128)(2,1)} async-done(((bf16[72,1440]{1,0:T(8,128)(2,1)}), bf16[4608,1440]{1,0:T(8,128)(2,1)}) %all-gather.3.cloned.1.call-update) | async-done | bytes 13271056 | tf_op jit(solution)/shard_map/all_gather | solution.py:414
  107.3 5.0 %shard_map.100 = f32[128,2560]{1,0:T(8,128)S(1)} custom-call(bf16[128,1440]{1,0:T(8,128)(2,1)S(1)} %copy.71.tokens_ref, f32[1,1440]{1,0:T(1,128)S(1)} %reshape.176.gain_ref, bf16[64,72,1440]{2,1,0:T(8,128)(2,1)} %bitcast.53), custom_call_target="tpu_custom_call" | custom-call | tf_op jit(solution)/shard_map/pallas_call | solution.py:266
  112.6 2.0 collective-permute-start
  115.1 2.1 collective-permute-start.1
  121.8 3.4 %shard_map.101 = (bf16[128,1440]{1,0:T(8,128)(2,1)S(1)}, bf16[128,1452]{1,0:T(8,128)(2,1)S(1)}) custom-call(bf16[128,2048]{1,0:T(8,128)(2,1)S(1)} %copy.82.attention_ref, bf16[64,72,1440]{2,1,0:T(8,128)(2,1)} %bitcast.54, bf16[128,1440]{1,0:T(8,128)(2,1)S(1)} %copy.71.tokens_ref, f32[1,1440]{1,0:T(1,128)S(1)} %reshape.179.gain_ref, ...), custom_call_target="tpu_custom_call" | custom-call | tf_op jit(solution)/shard_map/pallas_call | solution.py:310
  126.8 5.6 %collective-permute-done.3.refs_1_ = bf16[128,1452]{1,0:T(8,128)(2,1)S(1)} collective-permute-done((bf16[128,1452]{1,0:T(8,128)(2,1)S(1)}, bf16[128,1452]{1,0:T(8,128)(2,1)S(1)}, u32[]{:S(2)}, u32[]{:S(2)}) %collective-permute-start.3) | collective-permute-done | bytes 371744 | tf_op jit(solution)/shard_map/ppermute | solution.py:454
  132.4 1.9 collective-permute-start.5
  136.2 11.2 %all-to-all-start = ((bf16[8,16,1440]{2,1,0:T(8,128)(2,1)}), bf16[8,16,1440]{2,1,0:T(8,128)(2,1)S(1)}, u32[]{:S(2)}, u32[]{:S(2)}) async-start(bf16[8,16,1440]{2,1,0:T(8,128)(2,1)} %get-tuple-element.28), calls=%async_computation | async-start | bytes 786432 | tf_op jit(solution)/shard_map/all_to_all | solution.py:448
  147.3 3.0 collective-permute-start.7
  150.3 1.6 shard_map.103
  152.5 2.5 all-to-all-done.refs_0_
  155.0 4.7 %all-to-all-start.1 = ((bf16[8,32,1440]{2,1,0:T(8,128)(2,1)}), bf16[8,32,1440]{2,1,0:T(8,128)(2,1)S(1)}, u32[]{:S(2)}, u32[]{:S(2)}) async-start(bf16[8,32,1440]{2,1,0:T(8,128)(2,1)} %get-tuple-element.29), calls=%async_computation.1 | async-start | bytes 1572864 | tf_op jit(solution)/shard_map/all_to_all | solution.py:448
  159.7 3.0 %collective-permute-start.9 = (bf16[64,1452]{1,0:T(8,128)(2,1)S(1)}, bf16[64,1452]{1,0:T(8,128)(2,1)S(1)}, u32[]{:S(2)}, u32[]{:S(2)}) collective-permute-start(bf16[64,1452]{1,0:T(8,128)(2,1)S(1)} %slice.54), channel_id=1, source_target_pairs={{0,224},{32,0},{64,32},{96,64},{128,96},{160,128},{192,160},{224,1... | collective-permute-start | bytes 557576 | tf_op jit(solution)/shard_map/ppermute | solution.py:454
  162.9 3.8 %collective-permute-done.9 = bf16[64,1452]{1,0:T(8,128)(2,1)S(1)} collective-permute-done((bf16[64,1452]{1,0:T(8,128)(2,1)S(1)}, bf16[64,1452]{1,0:T(8,128)(2,1)S(1)}, u32[]{:S(2)}, u32[]{:S(2)}) %collective-permute-start.9) | collective-permute-done | bytes 185888 | tf_op jit(solution)/shard_map/ppermute | solution.py:454
  166.7 3.2 %collective-permute-done.8 = bf16[64,1452]{1,0:T(8,128)(2,1)S(1)} collective-permute-done((bf16[64,1452]{1,0:T(8,128)(2,1)S(1)}, bf16[64,1452]{1,0:T(8,128)(2,1)S(1)}, u32[]{:S(2)}, u32[]{:S(2)}) %collective-permute-start.8) | collective-permute-done | bytes 185888 | tf_op jit(solution)/shard_map/ppermute | solution.py:454
  169.9 2.0 shard_map.106
  171.9 5.9 %all-to-all-start.6 = ((bf16[8,48,1440]{2,1,0:T(8,128)(2,1)}), bf16[8,48,1440]{2,1,0:T(8,128)(2,1)S(1)}, u32[]{:S(2)}, u32[]{:S(2)}) async-start(bf16[8,48,1440]{2,1,0:T(8,128)(2,1)} %get-tuple-element.37), calls=%async_computation.6 | async-start | bytes 2359296 | tf_op jit(solution)/shard_map/all_to_all | solution.py:448
  179.4 14.8 %all-to-all-done.6.refs_0_ = bf16[8,48,1440]{2,1,0:T(8,128)(2,1)S(1)} async-done(((bf16[8,48,1440]{2,1,0:T(8,128)(2,1)}), bf16[8,48,1440]{2,1,0:T(8,128)(2,1)S(1)}, u32[]{:S(2)}, u32[]{:S(2)}) %all-to-all-start.6) | async-done | bytes 1105952 | tf_op jit(solution)/shard_map/all_to_all | solution.py:448
  194.2 4.4 %all-to-all-start.2 = ((bf16[8,32,1440]{2,1,0:T(8,128)(2,1)}), bf16[8,32,1440]{2,1,0:T(8,128)(2,1)S(1)}, u32[]{:S(2)}, u32[]{:S(2)}) async-start(bf16[8,32,1440]{2,1,0:T(8,128)(2,1)} %copy-done.1), calls=%async_computation.2 | async-start | bytes 1572864 | tf_op jit(solution)/shard_map/all_to_all | solution.py:448
  198.6 12.2 %shard_map.107 = bf16[8,48,1440]{2,1,0:T(8,128)(2,1)} custom-call(bf16[8,48,1440]{2,1,0:T(8,128)(2,1)S(1)} %all-to-all-done.6.refs_0_, bf16[1,1440,2880]{2,1,0:T(8,128)(2,1)} %refs_1_.1, bf16[1,1440,1440]{2,1,0:T(8,128)(2,1)} %refs_2_.1), custom_call_target="tpu_custom_call" | custom-call | tf_op jit(solution)/shard_map/pallas_call | solution.py:225
  210.9 4.8 %all-to-all-start.7 = ((bf16[8,48,1440]{2,1,0:T(8,128)(2,1)}), bf16[8,48,1440]{2,1,0:T(8,128)(2,1)S(1)}, u32[]{:S(2)}, u32[]{:S(2)}) async-start(bf16[8,48,1440]{2,1,0:T(8,128)(2,1)} %shard_map.107), calls=%async_computation.7 | async-start | bytes 2359296 | tf_op jit(solution)/shard_map/all_to_all | solution.py:448
  215.7 18.4 %shard_map.105 = (bf16[8,16,1440]{2,1,0:T(8,128)(2,1)S(1)}, bf16[8,32,1440]{2,1,0:T(8,128)(2,1)}, bf16[8,32,1440]{2,1,0:T(8,128)(2,1)S(1)}) custom-call(bf16[8,16,1440]{2,1,0:T(8,128)(2,1)S(1)} %all-to-all-done.refs_0_, bf16[8,32,1440]{2,1,0:T(8,128)(2,1)S(1)} %all-to-all-done.1.refs_1_, bf16[8,32,1440]{2,1,0:T(8,128)(2,1)S(1)} %all-to-all-done.2.refs_2_, ...), custom_call_target="tpu_custom_call" | custom-call | tf_op jit(solution)/shard_map/pallas_call | solution.py:225
  235.8 5.0 %all-to-all-start.5 = ((bf16[8,32,1440]{2,1,0:T(8,128)(2,1)}), bf16[8,32,1440]{2,1,0:T(8,128)(2,1)S(1)}, u32[]{:S(2)}, u32[]{:S(2)}) async-start(bf16[8,32,1440]{2,1,0:T(8,128)(2,1)} %copy-done), calls=%async_computation.5 | async-start | bytes 1572864 | tf_op jit(solution)/shard_map/all_to_all | solution.py:448
  241.0 1.5 collective-permute-start.10
  242.6 5.0 %collective-permute-done.10.rising_ref = bf16[64,1440]{1,0:T(8,128)(2,1)S(1)} collective-permute-done((bf16[64,1440]{1,0:T(8,128)(2,1)S(1)}, bf16[64,1440]{1,0:T(8,128)(2,1)S(1)}, u32[]{:S(2)}, u32[]{:S(2)}) %collective-permute-start.10) | collective-permute-done | bytes 184352 | tf_op jit(solution)/shard_map/ppermute | solution.py:454
  247.5 2.4 collective-permute-done.11.falling_ref
  252.9 5.8 %all-to-all-start.4 = ((bf16[8,32,1440]{2,1,0:T(8,128)(2,1)}), bf16[8,32,1440]{2,1,0:T(8,128)(2,1)S(1)}, u32[]{:S(2)}, u32[]{:S(2)}) async-start(bf16[8,32,1440]{2,1,0:T(8,128)(2,1)} %get-tuple-element.33), calls=%async_computation.4 | async-start | bytes 1572864 | tf_op jit(solution)/shard_map/all_to_all | solution.py:448
  258.7 2.1 collective-permute-done.12.rising_ref
  260.8 1.5 collective-permute-done.13.falling_ref
  264.9 5.9 %all-to-all-done.4.rows_ref = bf16[8,32,1440]{2,1,0:T(8,128)(2,1)S(1)} async-done(((bf16[8,32,1440]{2,1,0:T(8,128)(2,1)}), bf16[8,32,1440]{2,1,0:T(8,128)(2,1)S(1)}, u32[]{:S(2)}, u32[]{:S(2)}) %all-to-all-start.4) | async-done | bytes 737312 | tf_op jit(solution)/shard_map/all_to_all | solution.py:448
  275.7 15.0 %all_to_all.40.rows_ref = bf16[8,16,1440]{2,1,0:T(8,128)(2,1)S(1)} all-to-all(bf16[8,16,1440]{2,1,0:T(8,128)(2,1)S(1)} %copy-done.3), channel_id=1, replica_groups=mesh['z'=8,'y'=4,'c'=2,'x'=4] {'y','c'}, dimensions={0} | all-to-all | bytes 737280 | tf_op jit(solution)/shard_map/all_to_all | solution.py:448
  (103 shorter events, 33.4 us)
Async XLA Ops:
  6.5 100.8 %all-gather.3.cloned.1.call-start = ((), (), s32[]{:S(2)}) async-start(), calls=%async_computation.8 | async-start | bytes 14376960 | tf_op jit(solution)/shard_map/all_gather | solution.py:414
  112.6 7.8 %collective-permute-start = (bf16[128,4,64]{0,2,1:T(8,128)(2,1)S(1)}, bf16[128,4,64]{0,2,1:T(8,128)(2,1)S(1)}, u32[]{:S(2)}, u32[]{:S(2)}) collective-permute-start(bf16[128,4,64]{0,2,1:T(8,128)(2,1)S(1)} %bitcast.61), channel_id=1, source_target_pairs={{0,4},{4,8},{8,12},{12,16},{16,20},{20,24},{24,28},{28,32},{32,36}... | collective-permute-start | bytes 196616 | tf_op jit(solution)/shard_map/ppermute | solution.py:33
  115.1 3.5 %collective-permute-start.1 = (bf16[128,4,64]{0,2,1:T(8,128)(2,1)S(1)}, bf16[128,4,64]{0,2,1:T(8,128)(2,1)S(1)}, u32[]{:S(2)}, u32[]{:S(2)}) collective-permute-start(bf16[128,4,64]{0,2,1:T(8,128)(2,1)S(1)} %pad_maximum_fusion.2), channel_id=1, source_target_pairs={{0,4},{4,8},{8,12},{12,16},{16,20},{20,24},{24,28},{28,32},{32,36}... | collective-permute-start | bytes 196616 | tf_op jit(solution)/shard_map/ppermute | solution.py:33
  125.2 10.3 %copy-start.4 = (bf16[128,1440]{1,0:T(8,128)(2,1)}, bf16[128,1440]{1,0:T(8,128)(2,1)S(1)}, u32[]{:S(2)}) copy-start(bf16[128,1440]{1,0:T(8,128)(2,1)S(1)} %get-tuple-element.46.residual_ref) | copy-start | bytes 1105924
  125.3 7.2 %collective-permute-start.3 = (bf16[128,1452]{1,0:T(8,128)(2,1)S(1)}, bf16[128,1452]{1,0:T(8,128)(2,1)S(1)}, u32[]{:S(2)}, u32[]{:S(2)}) collective-permute-start(bf16[128,1452]{1,0:T(8,128)(2,1)S(1)} %get-tuple-element.26.refs_0_), channel_id=1, source_target_pairs={{0,224},{32,0},{64,32},{96,64},{128,96},{160,128},{192,160},{224,1... | collective-permute-start | bytes 1115144 | tf_op jit(solution)/shard_map/ppermute | solution.py:454
  126.4 7.8 %collective-permute-start.2 = (bf16[128,1452]{1,0:T(8,128)(2,1)S(1)}, bf16[128,1452]{1,0:T(8,128)(2,1)S(1)}, u32[]{:S(2)}, u32[]{:S(2)}) collective-permute-start(bf16[128,1452]{1,0:T(8,128)(2,1)S(1)} %get-tuple-element.26.refs_0_), channel_id=1, source_target_pairs={{0,32},{32,64},{64,96},{96,128},{128,160},{160,192},{192,224},{224... | collective-permute-start | bytes 1115144 | tf_op jit(solution)/shard_map/ppermute | solution.py:454
  132.4 14.9 %collective-permute-start.5 = (bf16[128,1452]{1,0:T(8,128)(2,1)S(1)}, bf16[128,1452]{1,0:T(8,128)(2,1)S(1)}, u32[]{:S(2)}, u32[]{:S(2)}) collective-permute-start(bf16[128,1452]{1,0:T(8,128)(2,1)S(1)} %collective-permute-done.3.refs_1_), channel_id=1, source_target_pairs={{0,224},{32,0},{64,32},{96,64},{128,96},{160,128},{192,160},{224,1... | collective-permute-start | bytes 1115144 | tf_op jit(solution)/shard_map/ppermute | solution.py:454
  134.3 16.0 %collective-permute-start.4 = (bf16[128,1452]{1,0:T(8,128)(2,1)S(1)}, bf16[128,1452]{1,0:T(8,128)(2,1)S(1)}, u32[]{:S(2)}, u32[]{:S(2)}) collective-permute-start(bf16[128,1452]{1,0:T(8,128)(2,1)S(1)} %collective-permute-done.2.refs_0_), channel_id=1, source_target_pairs={{0,32},{32,64},{64,96},{96,128},{128,160},{160,192},{192,224},{224... | collective-permute-start | bytes 1115144 | tf_op jit(solution)/shard_map/ppermute | solution.py:454
  136.2 18.9 %all-to-all-start = ((bf16[8,16,1440]{2,1,0:T(8,128)(2,1)}), bf16[8,16,1440]{2,1,0:T(8,128)(2,1)S(1)}, u32[]{:S(2)}, u32[]{:S(2)}) async-start(bf16[8,16,1440]{2,1,0:T(8,128)(2,1)} %get-tuple-element.28), calls=%async_computation | async-start | bytes 786432 | tf_op jit(solution)/shard_map/all_to_all | solution.py:448
  147.3 12.4 %collective-permute-start.7 = (bf16[128,1452]{1,0:T(8,128)(2,1)S(1)}, bf16[128,1452]{1,0:T(8,128)(2,1)S(1)}, u32[]{:S(2)}, u32[]{:S(2)}) collective-permute-start(bf16[128,1452]{1,0:T(8,128)(2,1)S(1)} %collective-permute-done.5.refs_1_), channel_id=1, source_target_pairs={{0,224},{32,0},{64,32},{96,64},{128,96},{160,128},{192,160},{224,1... | collective-permute-start | bytes 1115144 | tf_op jit(solution)/shard_map/ppermute | solution.py:454
  150.3 12.5 %collective-permute-start.6 = (bf16[128,1452]{1,0:T(8,128)(2,1)S(1)}, bf16[128,1452]{1,0:T(8,128)(2,1)S(1)}, u32[]{:S(2)}, u32[]{:S(2)}) collective-permute-start(bf16[128,1452]{1,0:T(8,128)(2,1)S(1)} %collective-permute-done.4.refs_0_), channel_id=1, source_target_pairs={{0,32},{32,64},{64,96},{96,128},{128,160},{160,192},{192,224},{224... | collective-permute-start | bytes 1115144 | tf_op jit(solution)/shard_map/ppermute | solution.py:454
  155.0 16.9 %all-to-all-start.1 = ((bf16[8,32,1440]{2,1,0:T(8,128)(2,1)}), bf16[8,32,1440]{2,1,0:T(8,128)(2,1)S(1)}, u32[]{:S(2)}, u32[]{:S(2)}) async-start(bf16[8,32,1440]{2,1,0:T(8,128)(2,1)} %get-tuple-element.29), calls=%async_computation.1 | async-start | bytes 1572864 | tf_op jit(solution)/shard_map/all_to_all | solution.py:448
  159.7 6.9 %collective-permute-start.9 = (bf16[64,1452]{1,0:T(8,128)(2,1)S(1)}, bf16[64,1452]{1,0:T(8,128)(2,1)S(1)}, u32[]{:S(2)}, u32[]{:S(2)}) collective-permute-start(bf16[64,1452]{1,0:T(8,128)(2,1)S(1)} %slice.54), channel_id=1, source_target_pairs={{0,224},{32,0},{64,32},{96,64},{128,96},{160,128},{192,160},{224,1... | collective-permute-start | bytes 557576 | tf_op jit(solution)/shard_map/ppermute | solution.py:454
  162.8 7.1 %collective-permute-start.8 = (bf16[64,1452]{1,0:T(8,128)(2,1)S(1)}, bf16[64,1452]{1,0:T(8,128)(2,1)S(1)}, u32[]{:S(2)}, u32[]{:S(2)}) collective-permute-start(bf16[64,1452]{1,0:T(8,128)(2,1)S(1)} %slice.53), channel_id=1, source_target_pairs={{0,32},{32,64},{64,96},{96,128},{128,160},{160,192},{192,224},{224... | collective-permute-start | bytes 557576 | tf_op jit(solution)/shard_map/ppermute | solution.py:454
  171.9 22.3 %all-to-all-start.6 = ((bf16[8,48,1440]{2,1,0:T(8,128)(2,1)}), bf16[8,48,1440]{2,1,0:T(8,128)(2,1)S(1)}, u32[]{:S(2)}, u32[]{:S(2)}) async-start(bf16[8,48,1440]{2,1,0:T(8,128)(2,1)} %get-tuple-element.37), calls=%async_computation.6 | async-start | bytes 2359296 | tf_op jit(solution)/shard_map/all_to_all | solution.py:448
  194.2 16.6 %all-to-all-start.2 = ((bf16[8,32,1440]{2,1,0:T(8,128)(2,1)}), bf16[8,32,1440]{2,1,0:T(8,128)(2,1)S(1)}, u32[]{:S(2)}, u32[]{:S(2)}) async-start(bf16[8,32,1440]{2,1,0:T(8,128)(2,1)} %copy-done.1), calls=%async_computation.2 | async-start | bytes 1572864 | tf_op jit(solution)/shard_map/all_to_all | solution.py:448
  210.9 24.9 %all-to-all-start.7 = ((bf16[8,48,1440]{2,1,0:T(8,128)(2,1)}), bf16[8,48,1440]{2,1,0:T(8,128)(2,1)S(1)}, u32[]{:S(2)}, u32[]{:S(2)}) async-start(bf16[8,48,1440]{2,1,0:T(8,128)(2,1)} %shard_map.107), calls=%async_computation.7 | async-start | bytes 2359296 | tf_op jit(solution)/shard_map/all_to_all | solution.py:448
  234.1 0.9 copy-start
  235.8 38.0 %copy-start.7 = (bf16[2,128,128]{2,1,0:T(8,128)(2,1)S(1)}, bf16[2,128,128]{2,1,0:T(8,128)(2,1)}, u32[]{:S(2)}) copy-start(bf16[2,128,128]{2,1,0:T(8,128)(2,1)} %copy-done.6) | copy-start | bytes 196612
  235.8 17.1 %all-to-all-start.5 = ((bf16[8,32,1440]{2,1,0:T(8,128)(2,1)}), bf16[8,32,1440]{2,1,0:T(8,128)(2,1)S(1)}, u32[]{:S(2)}, u32[]{:S(2)}) async-start(bf16[8,32,1440]{2,1,0:T(8,128)(2,1)} %copy-done), calls=%async_computation.5 | async-start | bytes 1572864 | tf_op jit(solution)/shard_map/all_to_all | solution.py:448
  240.8 34.9 %copy-start.3 = (bf16[8,16,1440]{2,1,0:T(8,128)(2,1)S(1)}, bf16[8,16,1440]{2,1,0:T(8,128)(2,1)}, u32[]{:S(2)}) copy-start(bf16[8,16,1440]{2,1,0:T(8,128)(2,1)} %copy-done.2) | copy-start | bytes 1105924
  240.8 49.9 %copy-start.5 = (bf16[128,1440]{1,0:T(8,128)(2,1)S(1)}, bf16[128,1440]{1,0:T(8,128)(2,1)}, u32[]{:S(2)}) copy-start(bf16[128,1440]{1,0:T(8,128)(2,1)} %copy-done.4) | copy-start | bytes 1105924
  240.8 49.9 %copy-start.9 = (bf16[1,128,128]{2,1,0:T(8,128)(2,1)S(1)}, bf16[1,128,128]{2,1,0:T(8,128)(2,1)}, u32[]{:S(2)}) copy-start(bf16[1,128,128]{2,1,0:T(8,128)(2,1)} %copy-done.8) | copy-start | bytes 98308
  241.0 6.5 %collective-permute-start.10 = (bf16[64,1440]{1,0:T(8,128)(2,1)S(1)}, bf16[64,1440]{1,0:T(8,128)(2,1)S(1)}, u32[]{:S(2)}, u32[]{:S(2)}) collective-permute-start(bf16[64,1440]{1,0:T(8,128)(2,1)S(1)} %get-tuple-element.38), channel_id=1, source_target_pairs={{0,224},{32,0},{64,32},{96,64},{128,96},{160,128},{192,160},{224,1... | collective-permute-start | bytes 552968 | tf_op jit(solution)/shard_map/ppermute | solution.py:454
  242.6 7.4 %collective-permute-start.11 = (bf16[64,1440]{1,0:T(8,128)(2,1)S(1)}, bf16[64,1440]{1,0:T(8,128)(2,1)S(1)}, u32[]{:S(2)}, u32[]{:S(2)}) collective-permute-start(bf16[64,1440]{1,0:T(8,128)(2,1)S(1)} %get-tuple-element.39), channel_id=1, source_target_pairs={{0,32},{32,64},{64,96},{96,128},{128,160},{160,192},{192,224},{224... | collective-permute-start | bytes 552968 | tf_op jit(solution)/shard_map/ppermute | solution.py:454
  251.1 9.7 %collective-permute-start.12 = (bf16[128,1440]{1,0:T(8,128)(2,1)}, bf16[128,1440]{1,0:T(8,128)(2,1)S(1)}, u32[]{:S(2)}, u32[]{:S(2)}) collective-permute-start(bf16[128,1440]{1,0:T(8,128)(2,1)} %get-tuple-element.40), channel_id=1, source_target_pairs={{0,224},{32,0},{64,32},{96,64},{128,96},{160,128},{192,160},{224,1... | collective-permute-start | bytes 1105928 | tf_op jit(solution)/shard_map/ppermute | solution.py:454
  251.4 10.9 %collective-permute-start.13 = (bf16[128,1440]{1,0:T(8,128)(2,1)}, bf16[128,1440]{1,0:T(8,128)(2,1)S(1)}, u32[]{:S(2)}, u32[]{:S(2)}) collective-permute-start(bf16[128,1440]{1,0:T(8,128)(2,1)} %get-tuple-element.41), channel_id=1, source_target_pairs={{0,32},{32,64},{64,96},{96,128},{128,160},{160,192},{192,224},{224... | collective-permute-start | bytes 1105928 | tf_op jit(solution)/shard_map/ppermute | solution.py:454
  252.9 17.9 %all-to-all-start.4 = ((bf16[8,32,1440]{2,1,0:T(8,128)(2,1)}), bf16[8,32,1440]{2,1,0:T(8,128)(2,1)S(1)}, u32[]{:S(2)}, u32[]{:S(2)}) async-start(bf16[8,32,1440]{2,1,0:T(8,128)(2,1)} %get-tuple-element.33), calls=%async_computation.4 | async-start | bytes 1572864 | tf_op jit(solution)/shard_map/all_to_all | solution.py:448
  263.4 8.9 %collective-permute-start.14 = (bf16[128,1440]{1,0:T(8,128)(2,1)}, bf16[128,1440]{1,0:T(8,128)(2,1)S(1)}, u32[]{:S(2)}, u32[]{:S(2)}) collective-permute-start(bf16[128,1440]{1,0:T(8,128)(2,1)} %get-tuple-element.42), channel_id=1, source_target_pairs={{0,224},{32,0},{64,32},{96,64},{128,96},{160,128},{192,160},{224,1... | collective-permute-start | bytes 1105928 | tf_op jit(solution)/shard_map/ppermute | solution.py:454
  263.7 10.1 %collective-permute-start.15 = (bf16[128,1440]{1,0:T(8,128)(2,1)}, bf16[128,1440]{1,0:T(8,128)(2,1)S(1)}, u32[]{:S(2)}, u32[]{:S(2)}) collective-permute-start(bf16[128,1440]{1,0:T(8,128)(2,1)} %get-tuple-element.43), channel_id=1, source_target_pairs={{0,32},{32,64},{64,96},{96,128},{128,160},{160,192},{192,224},{224... | collective-permute-start | bytes 1105928 | tf_op jit(solution)/shard_map/ppermute | solution.py:454
  274.1 16.5 %collective-permute-start.16 = (bf16[128,1440]{1,0:T(8,128)(2,1)S(1)}, bf16[128,1440]{1,0:T(8,128)(2,1)S(1)}, u32[]{:S(2)}, u32[]{:S(2)}) collective-permute-start(bf16[128,1440]{1,0:T(8,128)(2,1)S(1)} %get-tuple-element.44), channel_id=1, source_target_pairs={{0,224},{32,0},{64,32},{96,64},{128,96},{160,128},{192,160},{224,1... | collective-permute-start | bytes 1105928 | tf_op jit(solution)/shard_map/ppermute | solution.py:454
  274.5 16.2 %collective-permute-start.17 = (bf16[128,1440]{1,0:T(8,128)(2,1)S(1)}, bf16[128,1440]{1,0:T(8,128)(2,1)S(1)}, u32[]{:S(2)}, u32[]{:S(2)}) collective-permute-start(bf16[128,1440]{1,0:T(8,128)(2,1)S(1)} %get-tuple-element.45), channel_id=1, source_target_pairs={{0,32},{32,64},{64,96},{96,128},{128,160},{160,192},{192,224},{224... | collective-permute-start | bytes 1105928 | tf_op jit(solution)/shard_map/ppermute | solution.py:454
  (4 other events, 2.9 us)
Sparse Core Ops, SparseCore 0:
  10.1 97.2 all-gather.2
